TPU v7x, 32 devices: a whole 2x2x4 slice. The times are simulated.
32 devices in a mesh: dp: 8 (over y, x, core), tensor: 4 (over z).
Axes of the slice: x: 2, y: 2, z: 4, core: 2. Of those that a mesh axis runs over, the one named last changes fastest.
Arguments:
- tokens: bfloat16 [12288, 768], P('dp'), may hold values from -6 to 6
- lengths: int32 [8, 3], P('dp'), may hold values from 1 to 1024, 1536 in all within a row
- deal_order: int32 [12288], P('dp'), may hold values from 0 to 12287, as said below
- w_qkv: float32 [3, 768, 768], P(None, None, 'tensor'), may hold values from -0.21875 to 0.21875
- b_qv: float32 [2, 768], P(None, 'tensor'), may hold values from -3 to 3
- w_out: float32 [768, 768], P('tensor'), may hold values from -2.5 to 2.5
- b_out: float32 [768], replicated, may hold values from -2 to 2
- ln1_gain: float32 [768], replicated, may hold values from 0.5 to 1.5
- ln1_bias: float32 [768], replicated, may hold values from -2 to 2
- w_up: float32 [768, 3072], P(None, 'tensor'), may hold values from -0.21875 to 0.21875
- b_up: float32 [3072], P('tensor'), may hold values from -3 to 3
- w_down: float32 [3072, 768], P('tensor'), may hold values from -0.109375 to 0.109375
- b_down: float32 [768], replicated, may hold values from -2 to 2
- ln2_gain: float32 [768], replicated, may hold values from 0.5 to 1.5
- ln2_bias: float32 [768], replicated, may hold values from -2 to 2
- cotangent: bfloat16 [12288, 768], P('dp'), may hold values from -6 to 6
Outputs:
- output: bfloat16 [12288, 768], P('dp')
- input_grad: bfloat16 [12288, 768], P('dp')
- grad_w_qkv: float32 [3, 768, 768], P(None, None, 'tensor')
- grad_b_qv: float32 [2, 768], P(None, 'tensor')
- grad_w_out: float32 [768, 768], P('tensor')
- grad_b_out: float32 [768], replicated
- grad_ln1_gain: float32 [768], replicated
- grad_ln1_bias: float32 [768], replicated
- grad_w_up: float32 [768, 3072], P(None, 'tensor')
- grad_b_up: float32 [3072], P('tensor')
- grad_w_down: float32 [3072, 768], P('tensor')
- grad_b_down: float32 [768], replicated
- grad_ln2_gain: float32 [768], replicated
- grad_ln2_bias: float32 [768], replicated
Inputs may be any that keep to these rules, and one draw needn't show every extreme that they name: deal_order is a permutation of 0 to 12287. With b = 192, the token in row t of the s-th block of 1536 rows goes to a position p with (p mod 1536) // b equal to s. Each row of lengths sums to 1536.
All inputs are finite; a program needn't handle non-finite values.
Results may differ from a plain program's by a relative error of at most 0.02.
Values may be sent and summed in bfloat16 or wider, within the bound.
A program may use at most 128 MiB of HBM per device.

v0:
```python
import math

import jax
import jax.numpy as jnp
from jax import lax
from jax.sharding import PartitionSpec as P

HD = 64


def layer_norm(summed, gain_vec, bias_vec):
    average = jnp.mean(summed, axis=-1, keepdims=True)
    centered = summed - average
    variance = jnp.mean(centered * centered, axis=-1, keepdims=True)
    return centered * lax.rsqrt(variance + 1e-06) * gain_vec + bias_vec


def exact_gelu(values):
    return jax.nn.gelu(values, approximate=False)


def own_slice(rows, groups, pieces, part_index):
    width = rows.shape[1]
    sub_len = rows.shape[0] // (groups * pieces)
    shaped = rows.reshape(groups, pieces, sub_len, width)
    picked = lax.dynamic_slice_in_dim(shaped, part_index, 1, 1)
    return picked.reshape(groups * sub_len, width)


def to_owned(rows, groups, pieces):
    width = rows.shape[1]
    sub_len = rows.shape[0] // (groups * pieces)
    return rows.reshape(groups, pieces, sub_len, width).swapaxes(0, 1).reshape(rows.shape[0], width)


def from_owned(rows, groups, pieces):
    width = rows.shape[1]
    sub_len = rows.shape[0] // (groups * pieces)
    return rows.reshape(pieces, groups, sub_len, width).swapaxes(0, 1).reshape(rows.shape[0], width)


def on_device(
    tokens,
    lengths,
    deal_order,
    w_qkv,
    b_qv,
    w_out,
    b_out,
    ln1_gain,
    ln1_bias,
    w_up,
    b_up,
    w_down,
    b_down,
    ln2_gain,
    ln2_bias,
    cotangent,
):
    groups = lax.axis_size("dp")
    pieces = lax.axis_size("tensor")
    part_index = lax.axis_index("tensor")
    tok_count = tokens.shape[0]
    block_len = tok_count // groups
    sub_len = block_len // pieces
    local_heads = w_qkv.shape[2] // HD
    query_scale = HD ** (-0.5)
    slot_index = deal_order // tok_count * block_len + deal_order % block_len
    send_tokens = jnp.zeros_like(tokens).at[slot_index].set(tokens)
    send_cot = jnp.zeros_like(cotangent).at[slot_index].set(cotangent)
    got_tokens, got_cot = (
        lax.all_to_all(send_tokens, "dp", split_axis=0, concat_axis=0, tiled=True),
        lax.all_to_all(send_cot, "dp", split_axis=0, concat_axis=0, tiled=True),
    )
    dealt_owned = to_owned(got_tokens, groups, pieces)
    own_tokens = own_slice(got_tokens, groups, pieces, part_index)
    own_cot = own_slice(got_cot, groups, pieces, part_index)
    positions = jnp.arange(tok_count, dtype=jnp.int32)
    seq_ends = jnp.cumsum(lengths[0], dtype=jnp.int32)
    segment_id = jnp.sum((positions[:, None] >= seq_ends[None, :]).astype(jnp.int32), axis=1)
    wqkv_low = w_qkv.astype(jnp.bfloat16)
    bias_qv = b_qv.astype(jnp.bfloat16).astype(jnp.float32)
    wout_low = w_out.astype(jnp.bfloat16)
    bias_out = b_out.astype(jnp.bfloat16).astype(jnp.float32)
    wup_low = w_up.astype(jnp.bfloat16)
    bup_low = b_up.astype(jnp.bfloat16)
    wdown_low = w_down.astype(jnp.bfloat16)
    bias_down = b_down.astype(jnp.bfloat16).astype(jnp.float32)
    projected = jnp.einsum("td,cde->cte", got_tokens, wqkv_low, preferred_element_type=jnp.float32)
    query_low = (
        ((projected[0] + bias_qv[0]) * query_scale)
        .astype(jnp.bfloat16)
        .reshape(tok_count, local_heads, HD)
    )
    key_low = projected[1].astype(jnp.bfloat16).reshape(tok_count, local_heads, HD)
    value_low = (projected[2] + bias_qv[1]).astype(jnp.bfloat16).reshape(tok_count, local_heads, HD)
    row_block = math.gcd(512, tok_count)
    block_count = tok_count // row_block

    def block_scores(first_row):
        query_part = lax.dynamic_slice_in_dim(query_low, first_row, row_block, 0)
        segment_part = lax.dynamic_slice_in_dim(segment_id, first_row, row_block, 0)
        scores = jnp.einsum("qhd,khd->hqk", query_part, key_low, preferred_element_type=jnp.float32)
        same_doc = segment_part[:, None] == segment_id[None, :]
        return (query_part, jnp.where(same_doc[None], scores, -1000000000.0))

    def attend(block_index):
        query_part, scores = block_scores(block_index * row_block)
        row_max = jnp.max(scores, axis=-1, keepdims=True)
        exp_scores = jnp.exp(scores - row_max)
        row_total = jnp.sum(exp_scores, axis=-1, keepdims=True)
        probs_low = (exp_scores / row_total).astype(jnp.bfloat16)
        block_out = jnp.einsum(
            "hqk,khd->qhd", probs_low, value_low, preferred_element_type=jnp.float32
        )
        return (block_out.astype(jnp.bfloat16), row_max[..., 0] + jnp.log(row_total[..., 0]))

    attended_blocks, log_totals = lax.map(attend, jnp.arange(block_count, dtype=jnp.int32))
    attended = attended_blocks.reshape(tok_count, local_heads * HD)
    attended_owned = to_owned(attended, groups, pieces)
    picked = attended_owned
    attn_part = lax.psum_scatter(
        jnp.dot(picked, wout_low, preferred_element_type=jnp.float32),
        "tensor",
        scatter_dimension=0,
        tiled=True,
    )
    sum_first = attn_part + bias_out + own_tokens.astype(jnp.float32)
    hidden, first_back = jax.vjp(layer_norm, sum_first, ln1_gain, ln1_bias)
    hidden_low = hidden.astype(jnp.bfloat16)
    hidden_all = lax.all_gather(hidden_low, "tensor", axis=0, tiled=True)
    up_input = jnp.dot(hidden_all, wup_low, preferred_element_type=jnp.float32) + bup_low.astype(
        jnp.float32
    )
    activated, gelu_back = jax.vjp(exact_gelu, up_input)
    activated_low = activated.astype(jnp.bfloat16)
    picked = activated_low
    ffn_part = lax.psum_scatter(
        jnp.dot(picked, wdown_low, preferred_element_type=jnp.float32),
        "tensor",
        scatter_dimension=0,
        tiled=True,
    )
    sum_second = ffn_part + bias_down + hidden
    result, second_back = jax.vjp(layer_norm, sum_second, ln2_gain, ln2_bias)
    g_second, grad_ln2_gain, grad_ln2_bias = second_back(own_cot.astype(jnp.float32))
    grad_b_down = jnp.sum(g_second, axis=0)
    g_ffn_low = g_second.astype(jnp.bfloat16)
    g_ffn_all = lax.all_gather(g_ffn_low, "tensor", axis=0, tiled=True)
    (g_activated,) = gelu_back(jnp.dot(g_ffn_all, wdown_low.T, preferred_element_type=jnp.float32))
    g_up_low = g_activated.astype(jnp.bfloat16)
    grad_w_down = jnp.dot(activated_low.T, g_ffn_all, preferred_element_type=jnp.float32)
    grad_w_up = jnp.dot(hidden_all.T, g_up_low, preferred_element_type=jnp.float32)
    grad_b_up = jnp.sum(g_up_low.astype(jnp.float32), axis=0)
    picked = g_up_low
    g_hidden_ffn = lax.psum_scatter(
        jnp.dot(picked, wup_low.T, preferred_element_type=jnp.float32),
        "tensor",
        scatter_dimension=0,
        tiled=True,
    )
    g_hidden = g_second + g_hidden_ffn
    g_first, grad_ln1_gain, grad_ln1_bias = first_back(g_hidden)
    grad_b_out = jnp.sum(g_first, axis=0)
    g_attn_owned = lax.all_gather(g_first.astype(jnp.bfloat16), "tensor", axis=0, tiled=True)
    grad_w_out = jnp.dot(attended_owned.T, g_attn_owned, preferred_element_type=jnp.float32)
    g_attn_all = from_owned(g_attn_owned, groups, pieces)
    g_attended = (
        jnp.dot(g_attn_all, wout_low.T, preferred_element_type=jnp.float32)
        .astype(jnp.bfloat16)
        .reshape(tok_count, local_heads, HD)
    )

    def attend_back(carry, block_data):
        grad_key, grad_value = carry
        block_index, log_total = block_data
        first_row = block_index * row_block
        query_part, scores = block_scores(first_row)
        probs = jnp.exp(scores - log_total[..., None])
        probs_low = probs.astype(jnp.bfloat16)
        upstream = lax.dynamic_slice_in_dim(g_attended, first_row, row_block, 0)
        g_probs = jnp.einsum(
            "qhd,khd->hqk", upstream, value_low, preferred_element_type=jnp.float32
        )
        inner = jnp.sum(probs * g_probs, axis=-1, keepdims=True)
        g_scores = (probs * (g_probs - inner)).astype(jnp.bfloat16)
        g_query = jnp.einsum(
            "hqk,khd->qhd", g_scores, key_low, preferred_element_type=jnp.float32
        ).astype(jnp.bfloat16)
        grad_key = grad_key + jnp.einsum(
            "hqk,qhd->khd", g_scores, query_part, preferred_element_type=jnp.float32
        )
        grad_value = grad_value + jnp.einsum(
            "hqk,qhd->khd", probs_low, upstream, preferred_element_type=jnp.float32
        )
        return ((grad_key, grad_value), g_query)

    zero_state = jnp.zeros((tok_count, local_heads, HD), jnp.float32)
    (grad_key, grad_value), g_query_blocks = lax.scan(
        attend_back,
        (zero_state, zero_state),
        (jnp.arange(block_count, dtype=jnp.int32), log_totals),
    )
    g_stack = jnp.stack(
        [
            to_owned(g_query_blocks.reshape(tok_count, local_heads * HD), groups, pieces),
            to_owned(
                grad_key.reshape(tok_count, local_heads * HD).astype(jnp.bfloat16), groups, pieces
            ),
            to_owned(
                grad_value.reshape(tok_count, local_heads * HD).astype(jnp.bfloat16), groups, pieces
            ),
        ]
    )
    scale_vec = jnp.array([query_scale, 1.0, 1.0], jnp.float32)
    grad_w_qkv = (
        jnp.einsum("td,cte->cde", dealt_owned, g_stack, preferred_element_type=jnp.float32)
        * scale_vec[:, None, None]
    )
    grad_b_qv = jnp.stack(
        [
            query_scale * jnp.sum(g_stack[0].astype(jnp.float32), axis=0),
            jnp.sum(g_stack[2].astype(jnp.float32), axis=0),
        ]
    )
    scaled_weights = wqkv_low * jnp.array([query_scale, 1.0, 1.0], jnp.bfloat16)[:, None, None]
    picked = g_stack
    g_input_proj = lax.psum_scatter(
        jnp.einsum(
            "cte,cde->td", picked, scaled_weights, preferred_element_type=jnp.float32
        ).astype(jnp.bfloat16),
        "tensor",
        scatter_dimension=0,
        tiled=True,
    ).astype(jnp.float32)
    g_input_low = (g_first + g_input_proj).astype(jnp.bfloat16)
    back_result, back_input = (
        lax.all_to_all(result.astype(jnp.bfloat16), "dp", split_axis=0, concat_axis=0, tiled=True),
        lax.all_to_all(g_input_low, "dp", split_axis=0, concat_axis=0, tiled=True),
    )
    width = back_result.shape[1]
    full_result, full_input = (
        lax.all_gather(back_result.reshape(groups, sub_len, width), "tensor", axis=1, tiled=True),
        lax.all_gather(back_input.reshape(groups, sub_len, width), "tensor", axis=1, tiled=True),
    )
    output = full_result.reshape(tok_count, width)[slot_index]
    input_grad = full_input.reshape(tok_count, width)[slot_index]
    grad_w_qkv, grad_b_qv, grad_w_out, grad_w_up, grad_b_up, grad_w_down = lax.psum(
        (grad_w_qkv, grad_b_qv, grad_w_out, grad_w_up, grad_b_up, grad_w_down), "dp"
    )
    grad_b_out, grad_ln1_gain, grad_ln1_bias, grad_b_down, grad_ln2_gain, grad_ln2_bias = lax.psum(
        (grad_b_out, grad_ln1_gain, grad_ln1_bias, grad_b_down, grad_ln2_gain, grad_ln2_bias),
        ("dp", "tensor"),
    )
    return (
        output,
        input_grad,
        grad_w_qkv,
        grad_b_qv,
        grad_w_out,
        grad_b_out,
        grad_ln1_gain,
        grad_ln1_bias,
        grad_w_up,
        grad_b_up,
        grad_w_down,
        grad_b_down,
        grad_ln2_gain,
        grad_ln2_bias,
    )


def solution(mesh):
    placed = (
        P("dp", None),
        P("dp", None),
        P("dp"),
        P(None, None, "tensor"),
        P(None, "tensor"),
        P("tensor", None),
        P(),
        P(),
        P(),
        P(None, "tensor"),
        P("tensor"),
        P("tensor", None),
        P(),
        P(),
        P(),
        P("dp", None),
    )
    return jax.shard_map(
        on_device,
        mesh=mesh,
        in_specs=placed,
        out_specs=(
            P("dp", None),
            P("dp", None),
            P(None, None, "tensor"),
            P(None, "tensor"),
            P("tensor", None),
            P(),
            P(),
            P(),
            P(None, "tensor"),
            P("tensor"),
            P("tensor", None),
            P(),
            P(),
            P(),
        ),
        check_vma=False,
    )
```

profile of v0, /device:TPU:0, one launch (start us, length us, event | category | flops | bytes accessed | tf_op | source)
XLA Modules:
  0.0 924.4 jit_solution(1465354280746860340)
XLA Ops:
  7.9 9.7 %scatter_custom_fusion = bf16[1536,768]{1,0:T(8,128)(2,1)} fusion(s32[1536]{0:T(1024)S(1)} %compare_select_fusion, bf16[1536,768]{1,0:T(8,128)(2,1)} %param.22, bf16[]{:T(256)} %constant.40.clone.1), kind=kCustom, calls=%fused_computation.93 | custom fusion | bytes 2359808 | tf_op jit(solution)/shard_map/scatter | solution.py:69
  17.6 5.3 all-to-all-start
  25.0 27.3 %all-to-all-done = bf16[8,192,768]{2,1,0:T(8,128)(2,1)S(1)} async-done(((bf16[8,192,768]{2,1,0:T(8,128)(2,1)}), bf16[8,192,768]{2,1,0:T(8,128)(2,1)S(1)}, u32[]{:S(2)}, u32[]{:S(2)}) %all-to-all-start) | async-done | bytes 2359328 | tf_op jit(solution)/shard_map/all_to_all | solution.py:72
  54.5 28.7 %while.27 = (s32[]{:T(128)}, bf16[3,512,3,64]{1,3,2,0:T(8,128)(2,1)S(1)}, f32[3,3,512]{2,1,0:T(4,128)}, s32[3]{0:T(128)S(1)}, s32[1536]{0:T(1024)S(1)}, /*index=...) while((s32[]{:T(128)}, ...), condition=%wide.region_6.7_spmd, body=%wide.region_3.6_spmd.sunk | while | flops 626096640 | bytes 33097928 | solution.py:118
  96.7 83.0 %reduce-scatter.5.cloned.1.call-done = f32[384,768]{1,0:T(8,128)} async-done(((f32[1536,768]{1,0:T(8,128)}), f32[384,768]{1,0:T(8,128)}) %reduce-scatter.5.cloned.1.call-update) | async-done | bytes 1179664 | tf_op jit(solution)/shard_map/reduce_scatter | solution.py:122
  182.7 51.1 %all-gather.6.cloned.1.call-done = bf16[1536,768]{1,0:T(8,128)(2,1)} async-done(((bf16[384,768]{1,0:T(8,128)(2,1)}), bf16[1536,768]{1,0:T(8,128)(2,1)}) %all-gather.6.cloned.1.call-update) | async-done | bytes 2359312 | tf_op jit(solution)/shard_map/all_gather | solution.py:131
  233.8 15.6 %multiply_convert_fusion.1 = (bf16[1536,768]{1,0:T(8,128)(2,1)S(1)}, f32[1536,768]{1,0:T(8,128)}, f32[1536,768]{1,0:T(8,128)}) fusion(f32[768]{0:T(1024)S(1)} %convert_convert_fusion.1, bf16[1536,768]{1,0:T(8,128)(2,1)} %all-gather.6.cloned.1.call-done, f32[768,768]{1,0:T(8,128)} %param.31), kind=kOutput, calls=%fused_computation.51 | convolution fusion | flops 1890385920 | bytes 16518144 | tf_op jit(solution)/shard_map/dot_general | solution.py:132
  255.1 9.7 %scatter_custom_fusion.1 = bf16[1536,768]{1,0:T(8,128)(2,1)} fusion(s32[1536]{0:T(1024)} %copy-done.30, bf16[1536,768]{1,0:T(8,128)(2,1)} %param.37, bf16[]{:T(256)} %constant.40.clone.1), kind=kCustom, calls=%fused_computation.91 | custom fusion | bytes 2359808 | tf_op jit(solution)/shard_map/scatter | solution.py:70
  270.4 69.0 %reduce-scatter.7.cloned.1.call-done = f32[384,768]{1,0:T(8,128)} async-done(((f32[1536,768]{1,0:T(8,128)}), f32[384,768]{1,0:T(8,128)}) %reduce-scatter.7.cloned.1.call-update) | async-done | bytes 1179664 | tf_op jit(solution)/shard_map/reduce_scatter | solution.py:138
  351.2 51.1 %all-gather.10.cloned.1.call-done = bf16[1536,768]{1,0:T(8,128)(2,1)} async-done(((bf16[384,768]{1,0:T(8,128)(2,1)}), bf16[1536,768]{1,0:T(8,128)(2,1)}) %all-gather.10.cloned.1.call-update) | async-done | bytes 2359312 | tf_op jit(solution)/shard_map/all_gather | solution.py:149
  402.3 9.3 %convert_reduce_fusion = (f32[768]{0:T(1024)}, bf16[1536,768]{1,0:T(8,128)(2,1)S(1)}) fusion(f32[1536,768]{1,0:T(8,128)} %get-tuple-element.222, bf16[1536,768]{1,0:T(8,128)(2,1)} %all-gather.10.cloned.1.call-done, f32[768,768]{1,0:T(8,128)} %param.33, f32[1536,768]{1,0:T(8,128)} %get-tuple-element.236, f32[768]{0:T(1024)S(1)} %copy-done.46), kind=kOutput, calls=%fused_computation.49 | convolution fusion | flops 1832582400 | bytes 16521216 | tf_op jit(solution)/shard_map/dot_general | solution.py:150
  417.3 84.2 %reduce-scatter.9.cloned.1.call-done = f32[384,768]{1,0:T(8,128)} async-done(((f32[1536,768]{1,0:T(8,128)}), f32[384,768]{1,0:T(8,128)}) %reduce-scatter.9.cloned.1.call-update) | async-done | bytes 1179664 | tf_op jit(solution)/shard_map/reduce_scatter | solution.py:156
  508.6 51.1 %all-gather.12.cloned.1.call-done = bf16[1536,768]{1,0:T(8,128)(2,1)} async-done(((bf16[384,768]{1,0:T(8,128)(2,1)}), bf16[1536,768]{1,0:T(8,128)(2,1)}) %all-gather.12.cloned.1.call-update) | async-done | bytes 2359312 | tf_op jit(solution)/shard_map/all_gather | solution.py:165
  564.2 54.1 %while.28 = (s32[]{:T(128)}, f32[1536,3,64]{0,2,1:T(8,128)S(1)}, f32[1536,3,64]{0,2,1:T(8,128)S(1)}, bf16[3,512,3,64]{1,3,2,0:T(8,128)(2,1)}, s32[3]{0:T(128)S(1...) while((s32[]{:T(128)}, f32[1536,3,64]{0,2,1:T(8,128)S(1)}, ...), condition=%wide.region_21.22_spmd.clone, body=%wide.region_19.21_spmd.clone.sunk | while | flops 1540323840 | bytes 83814672 | solution.py:199
  636.8 5.2 bitcast_convert_fusion
  642.1 14.8 %all_to_all.39 = bf16[8,48,768]{2,1,0:T(8,128)(2,1)} all-to-all(bf16[8,48,768]{2,1,0:T(8,128)(2,1)} %bitcast.174), channel_id=1, replica_groups=mesh['dp'=8,'tensor'=4] {'dp'}, dimensions={0} | all-to-all | bytes 1179648 | tf_op jit(solution)/shard_map/all_to_all | solution.py:238
  656.9 32.1 %reduce-scatter.11.cloned.1.call-done = bf16[384,768]{1,0:T(8,128)(2,1)} async-done(((bf16[1536,768]{1,0:T(8,128)(2,1)}), bf16[384,768]{1,0:T(8,128)(2,1)}) %reduce-scatter.11.cloned.1.call-update) | async-done | bytes 589840 | tf_op jit(solution)/shard_map/reduce_scatter | solution.py:228
  690.3 14.0 %all_to_all.40 = bf16[8,48,768]{2,1,0:T(8,128)(2,1)} all-to-all(bf16[8,48,768]{2,1,0:T(8,128)(2,1)S(1)} %bitcast.173), channel_id=1, replica_groups=mesh['dp'=8,'tensor'=4] {'dp'}, dimensions={0} | all-to-all | bytes 1179648 | tf_op jit(solution)/shard_map/all_to_all | solution.py:239
  720.7 19.9 %all-gather.8.cloned.1.call-done = bf16[8,192,768]{2,1,0:T(8,128)(2,1)} async-done(((bf16[8,48,768]{2,1,0:T(8,128)(2,1)}), bf16[8,192,768]{2,1,0:T(8,128)(2,1)}) %all-gather.8.cloned.1.call-update) | async-done | bytes 2359312 | tf_op jit(solution)/shard_map/all_gather | solution.py:243
  740.6 8.7 gather_fusion
  749.3 43.3 %all-reduce = (f32[768]{0:T(1024)}, f32[768]{0:T(1024)}, f32[768]{0:T(1024)}, f32[768]{0:T(1024)}, f32[768]{0:T(1024)}, /*index=5*/f32[768]{0:T(1024)}) all-reduce(f32[768]{0:T(1024)S(1)} %copy-done.38, f32[768]{0:T(1024)S(1)} %copy-done.39, f32[768]{0:T(1024)S(1)} %copy-done.40, ...), channel_id=1, replica_groups=mesh['dp'=8,'tensor'=4] {'dp','tensor'}, use_global_device_ids=true, to_apply=%region_29.30 | all-reduce | flops 4608 | bytes 36864 | tf_op jit(solution)/shard_map/psum | solution.py:251
  794.3 14.2 %all-reduce.1 = (f32[2,192]{1,0:T(2,128)}, f32[768]{0:T(1024)}) all-reduce(f32[2,192]{1,0:T(2,128)S(1)} %pad_maximum_fusion.3, f32[768]{0:T(1024)S(1)} %copy-done.41), channel_id=1, replica_groups=mesh['dp'=8,'tensor'=4] {'dp'}, use_global_device_ids=true, to_apply=%region_26.27 | all-reduce | flops 1152 | bytes 9216 | tf_op jit(solution)/shard_map/psum | solution.py:248
  808.5 8.7 gather_fusion.1
  817.2 92.3 %all-reduce.5.cloned.1.call-done = (f32[3,768,192]{1,2,0:T(8,128)}, f32[192,768]{1,0:T(8,128)}, f32[768,768]{1,0:T(8,128)}, f32[768,768]{1,0:T(8,128)}) async-done(((f32[3,768,192]{1,2,0:T(8,128)}, f32[192,768]{1,0:T(8,128)}, f32[768,768]{1,0:T(8,128)}, f32[768,768]{1,0:T(8,128)}), (f32[3,768,192]{1,2,0:T(8,128)}, f32[192,768]{1,0:T(8,128)}, f32[768,768]{1,0:T(8,128)}, ...) | async-done | bytes 7077904 | tf_op jit(solution)/shard_map/psum | solution.py:248
  (262 shorter events, 185.4 us)
Async XLA Ops:
  17.6 34.8 %all-to-all-start = ((bf16[8,192,768]{2,1,0:T(8,128)(2,1)}), bf16[8,192,768]{2,1,0:T(8,128)(2,1)S(1)}, u32[]{:S(2)}, u32[]{:S(2)}) async-start(bf16[8,192,768]{2,1,0:T(8,128)(2,1)} %bitcast.158), calls=%async_computation | async-start | bytes 4718592 | tf_op jit(solution)/shard_map/all_to_all | solution.py:72
  22.9 156.8 %reduce-scatter.5.cloned.1.call-start = ((), (), s32[]{:S(2)}) async-start(), calls=%async_computation.8 | async-start | bytes 5898240 | tf_op jit(solution)/shard_map/reduce_scatter | solution.py:122
  24.9 29.0 %copy-start.22 = (bf16[3,768,192]{1,2,0:T(8,128)(2,1)}, bf16[3,768,192]{1,2,0:T(8,128)(2,1)S(1)}, u32[]{:S(2)}) copy-start(bf16[3,768,192]{1,2,0:T(8,128)(2,1)S(1)} %convert_element_type.144) | copy-start | bytes 2654212
  94.9 138.9 %all-gather.6.cloned.1.call-start = ((), (), s32[]{:S(2)}) async-start(), calls=%async_computation.9 | async-start | bytes 2949120 | tf_op jit(solution)/shard_map/all_gather | solution.py:131
  96.6 84.9 %copy-start.27 = (f32[768]{0:T(1024)S(1)}, f32[768]{0:T(1024)}, u32[]{:S(2)}) copy-start(f32[768]{0:T(1024)} %param.29) | copy-start | bytes 9220
  96.6 84.9 %copy-start.35 = (f32[768]{0:T(1024)S(1)}, f32[768]{0:T(1024)}, u32[]{:S(2)}) copy-start(f32[768]{0:T(1024)} %param.30) | copy-start | bytes 9220
  181.5 67.9 %copy-start.32 = (f32[384]{0:T(512)}, f32[384]{0:T(512)S(1)}, u32[]{:S(2)}) copy-start(f32[384]{0:T(512)S(1)} %multiply_reduce_fusion.4) | copy-start | bytes 4612
  181.5 67.9 %copy-start.28 = (f32[384]{0:T(512)}, f32[384]{0:T(512)S(1)}, u32[]{:S(2)}) copy-start(f32[384]{0:T(512)S(1)} %fusion.68) | copy-start | bytes 4612
  182.6 156.7 %reduce-scatter.7.cloned.1.call-start = ((), (), s32[]{:S(2)}) async-start(), calls=%async_computation.10 | async-start | bytes 5898240 | tf_op jit(solution)/shard_map/reduce_scatter | solution.py:138
  182.7 66.7 %copy-start.45 = (f32[768]{0:T(1024)}, f32[768]{0:T(1024)S(1)}, u32[]{:S(2)}) copy-start(f32[768]{0:T(1024)S(1)} %convert_convert_fusion.1) | copy-start | bytes 9220
  233.8 17.0 %copy-start.48 = (f32[768,768]{1,0:T(8,128)S(1)}, f32[768,768]{1,0:T(8,128)}, u32[]{:S(2)}) copy-start(f32[768,768]{1,0:T(8,128)} %param.33) | copy-start | bytes 7077892
  264.8 78.3 %all-to-all-start.2 = ((bf16[8,192,768]{2,1,0:T(8,128)(2,1)}), bf16[8,192,768]{2,1,0:T(8,128)(2,1)}, u32[]{:S(2)}, u32[]{:S(2)}) async-start(bf16[8,192,768]{2,1,0:T(8,128)(2,1)} %bitcast.159), calls=%async_computation.4 | async-start | bytes 4718592 | tf_op jit(solution)/shard_map/all_to_all | solution.py:73
  269.3 133.0 %all-gather.10.cloned.1.call-start = ((), (), s32[]{:S(2)}) async-start(), calls=%async_computation.12 | async-start | bytes 2949120 | tf_op jit(solution)/shard_map/all_gather | solution.py:149
  348.5 53.8 %copy-start.46 = (f32[768]{0:T(1024)S(1)}, f32[768]{0:T(1024)}, u32[]{:S(2)}) copy-start(f32[768]{0:T(1024)} %copy-done.45) | copy-start | bytes 9220
  348.5 63.1 %copy-start.34 = (f32[384]{0:T(512)}, f32[384]{0:T(512)S(1)}, u32[]{:S(2)}) copy-start(f32[384]{0:T(512)S(1)} %negate_multiply_fusion.2) | copy-start | bytes 4612
  351.1 150.4 %reduce-scatter.9.cloned.1.call-start = ((), (), s32[]{:S(2)}) async-start(), calls=%async_computation.13 | async-start | bytes 5898240 | tf_op jit(solution)/shard_map/reduce_scatter | solution.py:156
  417.2 84.3 %copy-start.6 = (f32[384,768]{1,0:T(8,128)S(1)}, f32[384,768]{1,0:T(8,128)}, u32[]{:S(2)}) copy-start(f32[384,768]{1,0:T(8,128)} %copy-done.5) | copy-start | bytes 3538948
  417.3 142.4 %all-gather.12.cloned.1.call-start = ((), (), s32[]{:S(2)}) async-start(), calls=%async_computation.14 | async-start | bytes 2949120 | tf_op jit(solution)/shard_map/all_gather | solution.py:165
  508.5 180.5 %reduce-scatter.11.cloned.1.call-start = ((), (), s32[]{:S(2)}) async-start(), calls=%async_computation.15 | async-start | bytes 2949120 | tf_op jit(solution)/shard_map/reduce_scatter | solution.py:228
  642.0 47.0 %copy-start.4 = (f32[384,768]{1,0:T(8,128)S(1)}, f32[384,768]{1,0:T(8,128)}, u32[]{:S(2)}) copy-start(f32[384,768]{1,0:T(8,128)} %copy-done.3) | copy-start | bytes 3538948
  642.0 98.5 %all-gather.8.cloned.1.call-start = ((), (), s32[]{:S(2)}) async-start(), calls=%async_computation.11 | async-start | bytes 2949120 | tf_op jit(solution)/shard_map/all_gather | solution.py:243
  656.8 151.7 %all-gather.14.cloned.1.call-start = ((), (), s32[]{:S(2)}) async-start(), calls=%async_computation.16 | async-start | bytes 2949120 | tf_op jit(solution)/shard_map/all_gather | solution.py:244
  704.3 205.1 %all-reduce.5.cloned.1.call-start = ((), (), s32[]{:S(2)}) async-start(), calls=%async_computation.17 | async-start | bytes 14155776 | tf_op jit(solution)/shard_map/psum | solution.py:248
  749.3 45.0 %copy-start.41 = (f32[768]{0:T(1024)S(1)}, f32[768]{0:T(1024)}, u32[]{:S(2)}) copy-start(f32[768]{0:T(1024)} %get-tuple-element.237) | copy-start | bytes 9220
  (43 other events, 153.2 us)
Sparse Core Ops, SparseCore 0:
  95.0 84.6 reduce-scatter.4
  182.8 50.9 all-gather.5
  255.2 84.0 reduce-scatter.6
  351.2 50.9 all-gather.9
  417.4 84.0 reduce-scatter.8
  508.6 50.9 all-gather.11
  642.1 46.8 reduce-scatter.10
  690.6 49.9 all-gather.7
  742.1 50.2 all-gather.13
  797.1 112.2 all-reduce.4
where the time goes:
time: 934 us; the launch traced here: 924 us
  waiting for transfers between devices  561 us (60%)
  matrix products  109 us (12%)
  local copies, waits for them, and re-layouts  90.2 us (10%)
  blocking collectives  86.4 us (9%)
  other arithmetic  47.6 us (5%)
  between operations  15.2 us (2%)
  starting transfers between devices  10.8 us (1%)
    psum x1, waiting for transfers between devices, on_device(): lax.psum((grad_w_qkv, grad_b_qv, grad_w_out, grad_w_up, grad_b_up, grad_w...  92.3 us
    reduce_scatter x1, waiting for transfers between devices, on_device(): lax.psum_scatter(jnp.dot(picked, wup_low.T, preferred_element_type=jnp.fl...  84.2 us
    reduce_scatter x1, waiting for transfers between devices, on_device(): lax.psum_scatter(jnp.dot(picked, wout_low, preferred_element_type=jnp.flo...  83 us
    reduce_scatter x1, waiting for transfers between devices, on_device(): lax.psum_scatter(jnp.dot(picked, wdown_low, preferred_element_type=jnp.fl...  69 us
    all_gather x1, waiting for transfers between devices, on_device(): g_ffn_all = lax.all_gather(g_ffn_low, 'tensor', axis=0, tiled=True)  51.1 us
    all_gather x1, waiting for transfers between devices, on_device(): lax.all_gather(g_first.astype(jnp.bfloat16), 'tensor', axis=0, tiled=True)  51.1 us
    all_gather x1, waiting for transfers between devices, on_device(): hidden_all = lax.all_gather(hidden_low, 'tensor', axis=0, tiled=True)  51.1 us
    psum x1, blocking collectives, on_device(): lax.psum((grad_b_out, grad_ln1_gain, grad_ln1_bias, grad_b_down, grad_ln2...  43.3 us
  transfers between devices with their start and end apart: 12, of which 10 were waited for; matrix products, arithmetic and copies ran while one was open for 5% of the time, Pallas kernels for 0%

commit v1 on v0

v1 whole, which is shorter than its diff:
```python
import functools
import math

import jax
import jax.numpy as jnp
from jax import lax
from jax.experimental import pallas as pl
from jax.experimental.pallas import tpu as pltpu
from jax.sharding import PartitionSpec as P

HD = 64
QUAD = 4
OCT = 8
BF = jnp.bfloat16
F32 = jnp.float32
MESH = pl.DeviceIdType.MESH
ANY = pl.BlockSpec(memory_space=pl.ANY)
VM = pl.BlockSpec(memory_space=pltpu.VMEM)
NEG = -1000000000.0


def params(limit=56, **kw):
    return pltpu.CompilerParams(vmem_limit_bytes=limit * 2**20, **kw)


def xs(a, k):
    if k & 1:
        a = a + 1 - 2 * (a % 2)
    if k & 2:
        a = a + 2 - 4 * ((a // 2) % 2)
    if k & 4:
        a = a + 4 - 8 * ((a // 4) % 2)
    return a


def xt(a, b):
    return (a + b) % 2 + 2 * ((a // 2 + b // 2) % 2)


def dot(a, b, ca=1, cb=0):
    return lax.dot_general(a, b, (((ca,), (cb,)), ((), ())), preferred_element_type=F32)


def pick_kernel(row_ref, tok_ref, cot_ref, tok_out, cot_out):
    rows = tok_out.shape[0]
    first = pl.program_id(0) * rows
    want = lax.broadcasted_iota(jnp.int32, (rows, 1), 0) + first
    hot = (want == row_ref[...]).astype(F32).astype(BF)
    tok_out[...] = dot(hot, tok_ref[...]).astype(BF)
    cot_out[...] = dot(hot, cot_ref[...]).astype(BF)


def pick_rows(row, tokens, cot, rows):
    n, width = tokens.shape
    blk = 128
    return pl.pallas_call(
        pick_kernel,
        grid=(rows // blk,),
        in_specs=[
            pl.BlockSpec((1, n), lambda i: (0, 0)),
            pl.BlockSpec((n, width), lambda i: (0, 0)),
            pl.BlockSpec((n, width), lambda i: (0, 0)),
        ],
        out_specs=[pl.BlockSpec((blk, width), lambda i: (i, 0))] * 2,
        out_shape=[jax.ShapeDtypeStruct((rows, width), BF)] * 2,
        compiler_params=params(),
        name="pick",
    )(row.reshape(1, n), tokens, cot)


def place_kernel(row_ref, rows_ref, out_ref):
    n = rows_ref.shape[0]
    blk = out_ref.shape[0]
    have = lax.broadcasted_iota(jnp.int32, (blk, n), 1)
    hot = (have == row_ref[...]).astype(F32).astype(BF)
    out_ref[...] = dot(hot, rows_ref[...]).astype(BF)


def place_rows(row, rows):
    n, width = rows.shape
    blk = 256
    return pl.pallas_call(
        place_kernel,
        grid=(n // blk,),
        in_specs=[
            pl.BlockSpec((blk, 1), lambda i: (i, 0)),
            pl.BlockSpec((n, width), lambda i: (0, 0)),
        ],
        out_specs=pl.BlockSpec((blk, width), lambda i: (i, 0)),
        out_shape=jax.ShapeDtypeStruct((n, width), BF),
        compiler_params=params(),
        name="place",
    )(row.reshape(n, 1), rows)


def deal_kernel(
    G, tok_ref, cot_ref, len_ref, wq_ref, bq_ref,
    xg_ref, cown_ref, len_out, wq_out, bq_out,
    s_a, r_a, s_b, r_b, s_c, r_c, s_d, r_d, s_e, r_e, s_f, r_f, loc,
):
    dp = lax.axis_index("dp")
    t = lax.axis_index("tensor")
    nq = G // QUAD
    m, par, quad, o = dp % 4, dp % 2, dp // 4, dp % 8
    base = dp - o

    def remote(src, dst, ss, rs, to_dp, to_t):
        return pltpu.make_async_remote_copy(
            src_ref=src, dst_ref=dst, send_sem=ss, recv_sem=rs,
            device_id=(to_dp, to_t), device_id_type=MESH,
        )

    def start(copy, local, is_self):
        @pl.when(is_self)
        def _():
            local.start()

        @pl.when(jnp.logical_not(is_self))
        def _():
            copy.start()

    sends_a = []
    for tp in range(4):
        for h in range(2):
            to = base + 4 * h + xs(t, tp)
            own = jnp.logical_and(to == dp, t == tp)
            copy = remote(wq_ref, wq_out.at[:, o], s_a.at[2 * tp + h], r_a.at[o], to, tp)
            local = pltpu.make_async_copy(wq_ref, wq_out.at[:, o], loc.at[0])
            start(copy, local, own)
            sends_a.append((copy, local, own))
    line = xt(m, t)
    copy_f = remote(bq_ref, bq_out, s_f, r_f, dp, line)
    local_f = pltpu.make_async_copy(bq_ref, bq_out, loc.at[1])
    own_f = m == 0
    start(copy_f, local_f, own_f)
    sends_e = []
    for j in range(4):
        copy = remote(len_ref, len_out, s_e.at[j], r_e, 4 * quad + j, t)
        local = pltpu.make_async_copy(len_ref, len_out, loc.at[2])
        own = m == j

        @pl.when(m == t)
        def _(copy=copy, local=local, own=own):
            start(copy, local, own)

        sends_e.append((copy, local, own))
    sends_b = []
    for q in range(nq):
        for k in range(2):
            to = 4 * q + par + 2 * k
            own = to == dp
            dst = xg_ref.at[dp // 2, par]
            copy = remote(tok_ref.at[q], dst, s_b.at[2 * q + k], r_b.at[dp // 2], to, t)
            local = pltpu.make_async_copy(tok_ref.at[q], dst, loc.at[3])
            start(copy, local, own)
            sends_b.append((copy, local, own))
    sends_d = []
    for q in range(nq):
        to = 4 * q + dp // nq
        own = to == dp
        dst = cown_ref.at[dp % nq]
        copy = remote(cot_ref.at[q], dst, s_d.at[q], r_d.at[dp % nq], to, t)
        local = pltpu.make_async_copy(cot_ref.at[q], dst, loc.at[4])
        start(copy, local, own)
        sends_d.append((copy, local, own))

    for s in range(G // 2):
        src = 2 * s + par
        dst = xg_ref.at[s, par]

        @pl.when(src != dp)
        def _(dst=dst, s=s, src=src):
            remote(tok_ref.at[0], dst, s_b.at[0], r_b.at[s], src, t).wait_recv()

        @pl.when(src == dp)
        def _(dst=dst):
            pltpu.make_async_copy(tok_ref.at[0], dst, loc.at[3]).wait()

    copy_c = remote(xg_ref.at[:, par], xg_ref.at[:, par], s_c, r_c, xs(dp, 1), t)
    copy_c.start()

    for copy, local, own in sends_a + [(copy_f, local_f, own_f)] + sends_b + sends_d:
        @pl.when(jnp.logical_not(own))
        def _(copy=copy):
            copy.wait_send()

    for copy, local, own in sends_e:
        @pl.when(jnp.logical_and(m == t, jnp.logical_not(own)))
        def _(copy=copy):
            copy.wait_send()

    for i in range(OCT):
        own = jnp.logical_and(o == i, m == 0)
        dst = wq_out.at[:, i]

        @pl.when(own)
        def _(dst=dst):
            pltpu.make_async_copy(wq_ref, dst, loc.at[0]).wait()

        @pl.when(jnp.logical_not(own))
        def _(dst=dst, i=i):
            remote(wq_ref, dst, s_a.at[0], r_a.at[i], base + i, line).wait_recv()

    @pl.when(own_f)
    def _():
        local_f.wait()

    @pl.when(jnp.logical_not(own_f))
    def _():
        copy_f.wait_recv()

    @pl.when(m == t)
    def _():
        pltpu.make_async_copy(len_ref, len_out, loc.at[2]).wait()

    @pl.when(m != t)
    def _():
        remote(len_ref, len_out, s_e.at[0], r_e, 4 * quad + t, t).wait_recv()

    for i in range(nq):
        src = m * nq + i
        dst = cown_ref.at[i]

        @pl.when(src != dp)
        def _(dst=dst, i=i, src=src):
            remote(cot_ref.at[0], dst, s_d.at[0], r_d.at[i], src, t).wait_recv()

        @pl.when(src == dp)
        def _(dst=dst):
            pltpu.make_async_copy(cot_ref.at[0], dst, loc.at[4]).wait()

    copy_c.wait()


def deal(G, tok, cot, lens, wq, bq):
    nq = G // QUAD
    b, width = tok.shape[1:]
    dma = pltpu.SemaphoreType.DMA
    return pl.pallas_call(
        functools.partial(deal_kernel, G),
        in_specs=[ANY] * 5,
        out_specs=[ANY] * 5,
        out_shape=[
            jax.ShapeDtypeStruct((G // 2, 2, b, width), BF),
            jax.ShapeDtypeStruct((nq, b, width), BF),
            jax.ShapeDtypeStruct(lens.shape, lens.dtype),
            jax.ShapeDtypeStruct((wq.shape[0], OCT) + wq.shape[1:], BF),
            jax.ShapeDtypeStruct(bq.shape, bq.dtype),
        ],
        scratch_shapes=[
            dma((8,)), dma((8,)), dma((2 * nq,)), dma((G // 2,)), dma, dma,
            dma((nq,)), dma((nq,)), dma((4,)), dma, dma, dma, dma((5,)),
        ],
        compiler_params=params(has_side_effects=True),
        name="deal",
    )(tok, cot, lens, wq, bq)


def doc_range(ends, row):
    first, last = 0, ends[-1]
    for e in ends[:-1]:
        first = jnp.where(row >= e, e, first)
    for e in reversed(ends[:-1]):
        last = jnp.where(row < e, e, last)
    return first, last


def segments(ends, rows):
    seg = jnp.zeros(rows.shape, jnp.int32)
    for e in ends[:-1]:
        seg = seg + (rows >= e).astype(jnp.int32)
    return seg


def read_ends(sc_ref, docs, total):
    ends, run = [], 0
    for d in range(docs - 1):
        run = run + sc_ref[d]
        ends.append(run)
    return ends + [total]


def half_mask(rows, upper):
    lane = lax.broadcasted_iota(jnp.int32, (rows, 2 * HD), 1)
    return (lane >= HD) if upper else (lane < HD)


def attn_fwd_kernel(docs, bq_rows, bk_rows, sc_ref, x_ref, w_ref, bias_ref, o0, o1, o2, o3, lse_ref, q_ref, k_ref, v_ref, o_s):
    n = x_ref.shape[0]
    own = o0.shape[0]
    m = lax.axis_index("dp") % 4
    scale = HD ** (-0.5)
    ends = read_ends(sc_ref, docs, n)

    def project(i, _):
        rows = pl.ds(pl.multiple_of(i * 256, 256), 256)
        xb = x_ref[rows, :]
        q_ref[rows, :] = ((dot(xb, w_ref[0]) + bias_ref[0:1, :]) * scale).astype(BF)
        k_ref[rows, :] = dot(xb, w_ref[1]).astype(BF)
        v_ref[rows, :] = (dot(xb, w_ref[2]) + bias_ref[1:2, :]).astype(BF)
        return 0

    lax.fori_loop(0, n // 256, project, 0)

    def q_block(i, _):
        r0 = pl.multiple_of(i * bq_rows, bq_rows)
        rows = pl.ds(r0, bq_rows)
        lo, _u = doc_range(ends, r0)
        _u, hi = doc_range(ends, r0 + bq_rows - 1)
        seg_q = segments(ends, r0 + lax.broadcasted_iota(jnp.int32, (bq_rows, 1), 0))
        qt = q_ref[rows, 0 : 2 * HD]
        zero = jnp.zeros_like(qt)
        qh = [
            jnp.where(half_mask(bq_rows, False), qt, zero),
            jnp.where(half_mask(bq_rows, True), qt, zero),
            q_ref[rows, 2 * HD : 3 * HD],
        ]

        def k_block(j, carry):
            k0 = pl.multiple_of(j * bk_rows, bk_rows)
            keys = pl.ds(k0, bk_rows)
            seg_k = segments(ends, k0 + lax.broadcasted_iota(jnp.int32, (1, bk_rows), 1))
            same = seg_q == seg_k
            out = []
            for h in range(3):
                cols = slice(0, 2 * HD) if h < 2 else slice(2 * HD, 3 * HD)
                mx, total, acc = carry[h]
                s = jnp.where(same, dot(qh[h], k_ref[keys, cols], 1, 1), NEG)
                new = jnp.maximum(mx, jnp.max(s, axis=1, keepdims=True))
                p = jnp.exp(s - new)
                alpha = jnp.exp(mx - new)
                total = alpha * total + jnp.sum(p, axis=1, keepdims=True)
                acc = alpha * acc + dot(p.astype(BF), v_ref[keys, cols])
                out.append((new, total, acc))
            return tuple(out)

        init = tuple(
            (
                jnp.full((bq_rows, 1), NEG, F32),
                jnp.zeros((bq_rows, 1), F32),
                jnp.zeros((bq_rows, 2 * HD if h < 2 else HD), F32),
            )
            for h in range(3)
        )
        res = lax.fori_loop(lo // bk_rows, (hi + bk_rows - 1) // bk_rows, k_block, init)
        heads = [acc / total for _m, total, acc in res]
        o_s[rows, 0 : 2 * HD] = jnp.where(half_mask(bq_rows, True), heads[1], heads[0]).astype(BF)
        o_s[rows, 2 * HD : 3 * HD] = heads[2].astype(BF)
        lane = lax.broadcasted_iota(jnp.int32, (bq_rows, 128), 1)
        stat = jnp.zeros((bq_rows, 128), F32)
        for h in range(3):
            mx, total, _a = res[h]
            stat = jnp.where(lane == h, mx + jnp.log(total), stat)
        lse_ref[rows, :] = stat
        return 0

    lax.fori_loop(0, n // bq_rows, q_block, 0)
    for j, ref in enumerate((o0, o1, o2, o3)):
        ref[...] = o_s[pl.ds(pl.multiple_of(xs(m, j) * own, own), own), :]


def attn_fwd(lens, x, w, bias):
    n = x.shape[0]
    wid = w.shape[2]
    own = n // QUAD
    sd = jax.ShapeDtypeStruct
    return pl.pallas_call(
        functools.partial(attn_fwd_kernel, lens.shape[0], 256, 256),
        in_specs=[pl.BlockSpec(memory_space=pltpu.SMEM), VM, VM, VM],
        out_specs=[VM] * 8,
        out_shape=[sd((own, wid), BF)] * 4 + [sd((n, 128), F32)] + [sd((n, wid), BF)] * 3,
        scratch_shapes=[pltpu.VMEM((n, wid), BF)],
        compiler_params=params(),
        name="attn_fwd",
    )(lens, x, w, bias)


def attn_bwd_kernel(
    docs, bq_rows, bk_rows, sc_ref, q_ref, k_ref, v_ref, lse_ref, o0, o1, o2, o3, d0, d1, d2, d3, w_ref,
    gq_ref, gk_ref, gv_ref, p0, p1, p2, p3, qm, km, dm, stat_s, dq_s,
):
    n = q_ref.shape[0]
    own = o0.shape[0]
    m = lax.axis_index("dp") % 4
    scale = HD ** (-0.5)
    ends = read_ends(sc_ref, docs, n)
    wide = 2 * HD

    for j, (oj, dj) in enumerate(((o0, d0), (o1, d1), (o2, d2), (o3, d3))):
        blk = own // 128

        def prep(i, _, oj=oj, dj=dj, j=j):
            src = pl.ds(pl.multiple_of(i * 128, 128), 128)
            dst = pl.ds(pl.multiple_of(xs(m, j) * own + i * 128, 128), 128)
            prod = oj[src, :].astype(F32) * dj[src, :].astype(F32)
            lane = lax.broadcasted_iota(jnp.int32, (128, 128), 1)
            stat = lse_ref[dst, :]
            low = half_mask(128, False)
            pt = prod[:, 0:wide]
            sums = [
                jnp.sum(jnp.where(low, pt, 0.0), axis=1, keepdims=True),
                jnp.sum(jnp.where(low, 0.0, pt), axis=1, keepdims=True),
                jnp.sum(prod[:, wide : wide + HD], axis=1, keepdims=True),
            ]
            for h in range(3):
                stat = jnp.where(lane == 3 + h, sums[h], stat)
            stat_s[:, dst] = stat.T[0:8, :]
            for ref, tile in ((qm, q_ref[dst, 0:wide]), (km, k_ref[dst, 0:wide]), (dm, dj[src, 0:wide])):
                zero = jnp.zeros_like(tile)
                ref[0, dst, :] = jnp.where(low, tile, zero)
                ref[1, dst, :] = jnp.where(low, zero, tile)
            pad = jnp.zeros((128, HD), BF)
            qm[2, dst, 0:HD] = q_ref[dst, wide : wide + HD]
            km[2, dst, 0:HD] = k_ref[dst, wide : wide + HD]
            dm[2, dst, 0:HD] = dj[src, wide : wide + HD]
            return 0

        lax.fori_loop(0, blk, prep, 0)

    dq_s[...] = jnp.zeros_like(dq_s)

    def k_block(j, _):
        k0 = pl.multiple_of(j * bk_rows, bk_rows)
        keys = pl.ds(k0, bk_rows)
        lo, _u = doc_range(ends, k0)
        _u, hi = doc_range(ends, k0 + bk_rows - 1)
        seg_k = segments(ends, k0 + lax.broadcasted_iota(jnp.int32, (bk_rows, 1), 0))

        def q_block(i, carry):
            r0 = pl.multiple_of(i * bq_rows, bq_rows)
            rows = pl.ds(r0, bq_rows)
            seg_q = segments(ends, r0 + lax.broadcasted_iota(jnp.int32, (1, bq_rows), 1))
            same = seg_k == seg_q
            st = stat_s[:, rows]
            dk, dv = list(carry[0]), list(carry[1])
            dq = [None, None]
            for h in range(3):
                tile = h // 2
                w = wide if h < 2 else HD
                kh = km[h, keys, 0:w]
                qh = qm[h, rows, 0:w]
                dh = dm[h, rows, 0:w]
                vh = v_ref[keys, 0:wide] if h < 2 else v_ref[keys, wide : wide + HD]
                s = jnp.where(same, dot(kh, qh, 1, 1), NEG)
                p = jnp.exp(s - st[h : h + 1, :])
                g = dot(vh, dh, 1, 1)
                ds = (p * (g - st[3 + h : 4 + h, :])).astype(BF)
                dv[tile] = dv[tile] + dot(p.astype(BF), dh)
                dk[tile] = dk[tile] + dot(ds, qh)
                part = dot(ds, kh, 0, 0)
                dq[tile] = part if dq[tile] is None else dq[tile] + part
            dq_s[rows, 0:wide] += dq[0]
            dq_s[rows, wide : wide + HD] += dq[1]
            return (tuple(dk), tuple(dv))

        zeros = (jnp.zeros((bk_rows, wide), F32), jnp.zeros((bk_rows, HD), F32))
        dk, dv = lax.fori_loop(lo // bq_rows, (hi + bq_rows - 1) // bq_rows, q_block, (zeros, zeros))
        gk_ref[keys, 0:wide] = dk[0].astype(BF)
        gk_ref[keys, wide : wide + HD] = dk[1].astype(BF)
        gv_ref[keys, 0:wide] = dv[0].astype(BF)
        gv_ref[keys, wide : wide + HD] = dv[1].astype(BF)
        return 0

    lax.fori_loop(0, n // bk_rows, k_block, 0)
    gq_ref[...] = (dq_s[...].astype(BF) * scale).astype(BF)

    for j, ref in enumerate((p0, p1, p2, p3)):
        rows = pl.ds(pl.multiple_of(xs(m, j) * own, own), own)
        ref[...] = (
            dot(gq_ref[rows, :], w_ref[0], 1, 1) + dot(gk_ref[rows, :], w_ref[1], 1, 1) + dot(gv_ref[rows, :], w_ref[2], 1, 1)
        ).astype(BF)


def attn_bwd(lens, q, k, v, lse, outs, grads, w):
    n, wid = q.shape
    own = n // QUAD
    width = w.shape[1]
    sd = jax.ShapeDtypeStruct
    return pl.pallas_call(
        functools.partial(attn_bwd_kernel, lens.shape[0], 256, 256),
        in_specs=[pl.BlockSpec(memory_space=pltpu.SMEM)] + [VM] * 13,
        out_specs=[VM] * 7,
        out_shape=[sd((n, wid), BF)] * 3 + [sd((own, width), BF)] * 4,
        scratch_shapes=[
            pltpu.VMEM((3, n, 2 * HD), BF), pltpu.VMEM((3, n, 2 * HD), BF), pltpu.VMEM((3, n, 2 * HD), BF),
            pltpu.VMEM((8, n), F32), pltpu.VMEM((n, wid), F32),
        ],
        compiler_params=params(),
        name="attn_bwd",
    )(lens, q, k, v, lse, *outs, *grads, w)


def quad_kernel(n_pair, *refs):
    src = refs[0:3]
    pair_in = refs[3 : 3 + n_pair]
    dst = refs[3 + n_pair : 6 + n_pair]
    pair_out = refs[6 + n_pair : 6 + 2 * n_pair]
    ss, rs = refs[6 + 2 * n_pair :]
    dp = lax.axis_index("dp")
    t = lax.axis_index("tensor")
    copies = []
    for i in range(3 + n_pair):
        a, b, k = (src[i], dst[i], i + 1) if i < 3 else (pair_in[i - 3], pair_out[i - 3], 1)
        copies.append(
            pltpu.make_async_remote_copy(
                src_ref=a, dst_ref=b, send_sem=ss.at[i], recv_sem=rs.at[i],
                device_id=(xs(dp, k), t), device_id_type=MESH,
            )
        )
    for i in (1, 2, 0):
        copies[i].start()
    for i in range(3, 3 + n_pair):
        copies[i].start()
    for c in copies:
        c.wait()


def quad_exchange(pieces, pair):
    every = list(pieces) + list(pair)
    dma = pltpu.SemaphoreType.DMA
    out = pl.pallas_call(
        functools.partial(quad_kernel, len(pair)),
        in_specs=[ANY] * len(every),
        out_specs=[ANY] * len(every),
        out_shape=[jax.ShapeDtypeStruct(a.shape, a.dtype) for a in every],
        scratch_shapes=[dma((len(every),)), dma((len(every),))],
        compiler_params=params(has_side_effects=True),
        name="quad",
    )(*every)
    return out[:3], out[3:]


def gelu_parts(v):
    z = jnp.abs(v)
    u = 1.0 / (1.0 + (0.3275911 * math.sqrt(0.5)) * z)
    e = jnp.exp(-0.5 * v * v)
    poly = u * (0.5 * 0.254829592 + u * (0.5 * -0.284496736 + u * (0.5 * 1.421413741 + u * (0.5 * -1.453152027 + u * (0.5 * 1.061405429)))))
    tail = poly * e
    phi = jnp.where(v >= 0.0, 1.0 - tail, tail)
    return v * phi, phi + v * e * (1.0 / math.sqrt(2.0 * math.pi))


def ffn_kernel(
    ch, ch_o, nsem,
    a0, a1, a2, a3, x_any, cot_ref, vb_out, vg1, vb1, vb_down, vg2, vb2,
    wu_own, wd_own, wo_own, bu_own,
    z1, c1, y1, e1, z2, c2, y2, e2, sz1, sc1, sy1, se1, sz2, sc2, sy2, se2,
    res_ref, gfirst_ref, gat0, gat1, gat2, gat3, act_ref, gup_ref, hid_ref, gffn_ref, gattn_ref, vec_ref, gbup_ref,
    wu, wd, wo, bu, xo, gp, sem,
):
    dp = lax.axis_index("dp")
    t = lax.axis_index("tensor")
    m, o = dp % 4, dp % 8
    own, width = res_ref.shape
    count = [0]
    copies = {"o": [], "u": [], "d": []}

    def load(kind, src, dst):
        c = pltpu.make_async_copy(src, dst, sem.at[count[0]])
        count[0] += 1
        c.start()
        copies[kind].append(c)

    load("o", x_any.at[pl.ds(pl.multiple_of(m * own, own), own), :], xo)
    load("o", wo_own, wo.at[t])
    for arr, k in ((z1, 0), (sz1, 1), (c1, 2), (sc1, 3)):
        for j in (1, 2, 3):
            dst = wo.at[xs(t, j), pl.ds(pl.multiple_of(xs(m, k) * ch_o, ch_o), ch_o), :]
            load("o", arr.at[j - 1, pl.ds(ch + 16, ch_o), :], dst)
    load("u", wu_own, wu.at[t])
    load("u", bu_own, bu.at[t])
    for j in (1, 2, 3):
        load("u", z1.at[j - 1, pl.ds(ch, 16), :], bu.at[xs(t, j)])
    for kind, w, arrs in (
        ("u", wu, (z1, sz1, c1, sc1, y1, sy1, e1, se1)),
        ("d", wd, (z2, sz2, c2, sc2, y2, sy2, e2, se2)),
    ):
        if kind == "d":
            load("d", wd_own, wd.at[t])
        for k, arr in enumerate(arrs):
            for j in (1, 2, 3):
                dst = w.at[xs(t, j), pl.ds(pl.multiple_of(xs(o, k) * ch, ch), ch), :]
                load(kind, arr.at[j - 1, pl.ds(0, ch), :], dst)

    for c in copies["o"]:
        c.wait()
    attn = jnp.zeros((own, width), F32)
    for j, a in enumerate((a0, a1, a2, a3)):
        attn = attn + dot(a[...], wo[xt(xs(m, j), t)])

    def norm(z):
        mean = jnp.mean(z, axis=1, keepdims=True)
        c = z - mean
        var = jnp.mean(c * c, axis=1, keepdims=True)
        r = lax.rsqrt(var + 1e-06)
        return c * r, r

    n1, r1 = norm(attn + vb_out[...].astype(BF).astype(F32) + xo[...].astype(F32))
    hidden = n1 * vg1[...] + vb1[...]
    hid_ref[...] = hidden.astype(BF)
    for c in copies["u"]:
        c.wait()
    for c in copies["d"]:
        c.wait()

    sub = 256

    def forward(s, acc):
        for p in range(width // sub):
            cols = slice(p * sub, (p + 1) * sub)
            up = dot(hid_ref[...], wu[s, :, cols]) + bu[s, 0:1, cols].astype(F32)
            act, grad = gelu_parts(up)
            act_ref[s, :, cols] = act.astype(BF)
            gp[s, :, cols] = grad
            acc = acc + dot(act.astype(BF), wd[s, cols, :])
        return acc

    ffn = lax.fori_loop(0, 4, forward, jnp.zeros((own, width), F32))
    n2, r2 = norm(ffn + vb_down[...].astype(BF).astype(F32) + hidden)
    res_ref[...] = (n2 * vg2[...] + vb2[...]).astype(BF)
    e = cot_ref[...].astype(F32)

    def norm_back(e, n, r, gain):
        eg = e * gain
        return r * (eg - jnp.mean(eg, axis=1, keepdims=True) - n * jnp.mean(eg * n, axis=1, keepdims=True))

    g_second = norm_back(e, n2, r2, vg2[...])
    vec_ref[...] = jnp.zeros_like(vec_ref)
    vec_ref[4:5, :] = jnp.sum(e * n2, axis=0, keepdims=True)
    vec_ref[5:6, :] = jnp.sum(e, axis=0, keepdims=True)
    vec_ref[3:4, :] = jnp.sum(g_second, axis=0, keepdims=True)
    gffn_ref[...] = g_second.astype(BF)

    def backward(s, acc):
        for p in range(width // sub):
            cols = slice(p * sub, (p + 1) * sub)
            g = (dot(gffn_ref[...], wd[s, cols, :], 1, 1) * gp[s, :, cols]).astype(BF)
            gup_ref[s, :, cols] = g
            gbup_ref[s, 0:1, cols] = jnp.sum(g.astype(F32), axis=0, keepdims=True)
            acc = acc + dot(g, wu[s, :, cols], 1, 1)
        return acc

    g_hidden = lax.fori_loop(0, 4, backward, g_second)
    g_first = norm_back(g_hidden, n1, r1, vg1[...])
    vec_ref[1:2, :] = jnp.sum(g_hidden * n1, axis=0, keepdims=True)
    vec_ref[2:3, :] = jnp.sum(g_hidden, axis=0, keepdims=True)
    vec_ref[0:1, :] = jnp.sum(g_first, axis=0, keepdims=True)
    gfirst_ref[...] = g_first
    gattn_ref[...] = g_first.astype(BF)
    for j, ref in enumerate((gat0, gat1, gat2, gat3)):
        ref[...] = dot(gattn_ref[...], wo[xt(xs(m, j), t)], 1, 1).astype(BF)


def ffn(att, x, cot, vecs, owns, pieces):
    own, wid = att[0].shape
    width = cot.shape[1]
    ch, ch_o = width // OCT, wid // QUAD
    sd = jax.ShapeDtypeStruct
    nsem = 2 + 12 + 2 + 3 + 24 + 1 + 24
    return pl.pallas_call(
        functools.partial(ffn_kernel, ch, ch_o, nsem),
        in_specs=[VM] * 4 + [ANY] + [VM] * 7 + [ANY] * (4 + 16),
        out_specs=[VM] * 13,
        out_shape=[
            sd((own, width), BF), sd((own, width), F32),
            sd((own, wid), BF), sd((own, wid), BF), sd((own, wid), BF), sd((own, wid), BF),
            sd((4, own, width), BF), sd((4, own, width), BF),
            sd((own, width), BF), sd((own, width), BF), sd((own, width), BF),
            sd((8, width), F32), sd((4, 1, width), F32),
        ],
        scratch_shapes=[
            pltpu.VMEM((4, width, width), BF), pltpu.VMEM((4, width, width), BF), pltpu.VMEM((4, wid, width), BF),
            pltpu.VMEM((4, 16, width), BF), pltpu.VMEM((own, width), BF), pltpu.VMEM((4, own, width), F32),
            pltpu.SemaphoreType.DMA((nsem,)),
        ],
        compiler_params=params(60),
        name="ffn",
    )(*att, x, cot, *vecs, *owns, *pieces)


def wgrad_kernel(a0, a1, a2, a3, act_ref, gup_ref, hid_ref, gffn_ref, gattn_ref, du_ref, dd_ref, do_ref):
    m = lax.axis_index("dp") % 4
    t = lax.axis_index("tensor")

    def one(s, _):
        dd_ref[s] = dot(act_ref[s], gffn_ref[...], 0, 0).astype(BF)
        du_ref[s] = dot(hid_ref[...], gup_ref[s], 0, 0).astype(BF)
        return 0

    lax.fori_loop(0, 4, one, 0)
    for j, a in enumerate((a0, a1, a2, a3)):
        do_ref[xt(xs(m, j), t)] = dot(a[...], gattn_ref[...], 0, 0).astype(BF)


def wgrad(att, act, gup, hid, gffn, gattn):
    wid = att[0].shape[1]
    width = hid.shape[1]
    sd = jax.ShapeDtypeStruct
    return pl.pallas_call(
        wgrad_kernel,
        in_specs=[VM] * 9,
        out_specs=[VM] * 3,
        out_shape=[sd((4, width, width), BF), sd((4, width, width), BF), sd((4, wid, width), BF)],
        compiler_params=params(),
        name="wgrad",
    )(*att, act, gup, hid, gffn, gattn)


def on_device(
    tokens, lengths, deal_order, w_qkv, b_qv, w_out, b_out, ln1_gain, ln1_bias,
    w_up, b_up, w_down, b_down, ln2_gain, ln2_bias, cotangent,
):
    G = lax.axis_size("dp")
    T = lax.axis_size("tensor")
    dp = lax.axis_index("dp")
    t = lax.axis_index("tensor")
    n, width = tokens.shape
    b = n // G
    nq = G // QUAD
    own = n // QUAD
    wid = w_qkv.shape[2]
    ch, ch_o = width // OCT, wid // QUAD
    docs = lengths.shape[1]
    m, o, quad = dp % 4, dp % 8, dp // 4

    dpp = lambda x, k: lax.ppermute(x, "dp", [(i, i ^ k) for i in range(G)])
    zpp = lambda x, k: lax.ppermute(x, "tensor", [(i, i ^ k) for i in range(T)])

    group, slot = deal_order // n, deal_order % b
    q_of, t_of = group // T, group % T
    send_row = jnp.where(t_of == t, q_of * b + slot, -1)
    back_row = t_of * own + ((dp % nq - q_of) % nq) * b + slot
    tok_s, cot_s = pick_rows(send_row, tokens, cotangent, own)

    cut = lambda w, start, rows: lax.dynamic_slice_in_dim(w, start, rows, 0).astype(BF)
    bu16 = jnp.broadcast_to(b_up.astype(BF)[None], (16, width))
    first = jnp.concatenate([cut(w_up, o * ch, ch), bu16, cut(w_out, m * ch_o, ch_o)])
    second = cut(w_down, o * ch, ch)
    z1 = jnp.stack([zpp(first, k) for k in (1, 2, 3)])
    z2 = jnp.stack([zpp(second, k) for k in (1, 2, 3)])
    c1, y1 = dpp(z1, 2), dpp(z1[:, :ch], 4)
    e1 = dpp(y1, 2)
    c2, y2 = dpp(z2, 2), dpp(z2, 4)
    e2 = dpp(c2, 4)

    wq_c = lax.dynamic_slice_in_dim(w_qkv, o * ch, ch, 1).astype(BF)
    bq = jnp.zeros((8, wid), F32).at[:2].set(b_qv.astype(BF).astype(F32))
    lens = jnp.zeros((8, 128), jnp.int32).at[0, :docs].set(lengths[0])
    xg, cown, lens_g, wq, bq_g = deal(G, tok_s.reshape(nq, b, width), cot_s.reshape(nq, b, width), lens, wq_c, bq)
    xg = xg.reshape(n, width)
    cown = cown.reshape(own, width)
    wq = wq.reshape(3, width, wid)
    lens3 = lens_g[0, :docs]

    a0, a1, a2, a3, lse, q, k, v = attn_fwd(lens3, xg, wq, bq_g)
    (b1, b2, b3), pair = quad_exchange((a1, a2, a3), (z1, c1, y1, e1, z2, c2, y2, e2))

    row = lambda vec: vec.reshape(1, width)
    vecs = [row(u) for u in (b_out, ln1_gain, ln1_bias, b_down, ln2_gain, ln2_bias)]
    owns = [w_up.astype(BF), w_down.astype(BF), w_out.astype(BF), bu16]
    att = (a0, b1, b2, b3)
    (result, g_first, ga0, ga1, ga2, ga3, act, gup, hid, gffn, gattn, vec, gbup) = ffn(
        att, xg, cown, vecs, owns, [z1, c1, y1, e1, z2, c2, y2, e2] + list(pair)
    )

    def send_back(rows):
        blocks = rows.reshape(nq, b, width)
        got = []
        for s in range(nq):
            pick = lax.dynamic_index_in_dim(blocks, (quad + s) % nq, 0, False)
            perm = [(4 * qq + mm, mm * nq + (qq + s) % nq) for qq in range(nq) for mm in range(4)]
            got.append(lax.ppermute(pick, "dp", perm))
        mine = jnp.concatenate(got)
        return lax.all_gather(mine, "tensor", axis=0, tiled=True)

    h1, h2, h3 = (dpp(g, i) for g, i in ((ga1, 1), (ga2, 2), (ga3, 3)))
    out_rows = send_back(result)
    du, dd, do = wgrad(att, act, gup, hid, gffn, gattn)

    gq, gk, gv, p0, p1, p2, p3 = attn_bwd(lens3, q, k, v, lse, (a0, a1, a2, a3), (ga0, h1, h2, h3), wq)
    s0 = p0.astype(F32) + dpp(p1, 1).astype(F32)
    s2 = (p2.astype(F32) + dpp(p3, 1).astype(F32)).astype(BF)
    g_low = (g_first + s0 + dpp(s2, 2).astype(F32)).astype(BF)
    in_rows = send_back(g_low)

    output = place_rows(back_row, out_rows)
    input_grad = place_rows(back_row, in_rows)

    octs = [[OCT * i + j for j in range(OCT)] for i in range(G // OCT)]
    across = [[OCT * i + j for i in range(G // OCT)] for j in range(OCT)]

    def reduce_weight(part):
        rows = part.shape[1]
        split = part.reshape(4, OCT, rows // OCT, width).swapaxes(0, 1)
        mine = lax.psum_scatter(split, "dp", scatter_dimension=0, axis_index_groups=octs, tiled=True)
        if G > OCT:
            mine = lax.psum(mine, "dp", axis_index_groups=across)
        mine = lax.psum_scatter(mine[0], "tensor", scatter_dimension=0, tiled=True)
        full = lax.all_gather(mine[0], "dp", axis=0, axis_index_groups=octs, tiled=True)
        return full.astype(F32)

    grad_w_up = reduce_weight(du)
    grad_w_down = reduce_weight(dd)
    grad_w_out = reduce_weight(do)
    g3 = jnp.stack([gq, gk, gv])
    dqkv = jnp.einsum("td,cte->cde", xg, g3, preferred_element_type=F32).astype(BF)
    perm = [(d * T + tt, d * T + ((d % 4) ^ tt)) for d in range(G) for tt in range(T)]
    dqkv = lax.ppermute(dqkv, ("dp", "tensor"), perm)
    grad_w_qkv = lax.psum(dqkv, "dp").astype(F32)
    db = jnp.stack([jnp.sum(gq.astype(F32), 0), jnp.sum(gv.astype(F32), 0)])
    db = lax.ppermute(db, ("dp", "tensor"), perm)
    slot_db = jnp.zeros((T, 2, wid), F32)
    slot_db = lax.dynamic_update_index_in_dim(slot_db, db, t, 0)
    small = jnp.concatenate([vec[:6].reshape(-1), gbup.reshape(-1), slot_db.reshape(-1)])
    small = lax.psum(small, ("dp", "tensor"))
    vec = small[: 6 * width].reshape(6, width)
    grad_b_up = lax.dynamic_slice_in_dim(small, 6 * width + t * width, width)
    grad_b_qv = lax.dynamic_slice_in_dim(small, (6 + T) * width + t * 2 * wid, 2 * wid).reshape(2, wid)
    return (
        output, input_grad, grad_w_qkv, grad_b_qv, grad_w_out, vec[0], vec[1], vec[2],
        grad_w_up, grad_b_up, grad_w_down, vec[3], vec[4], vec[5],
    )


def solution(mesh):
    placed = (
        P("dp", None), P("dp", None), P("dp"), P(None, None, "tensor"), P(None, "tensor"), P("tensor", None),
        P(), P(), P(), P(None, "tensor"), P("tensor"), P("tensor", None), P(), P(), P(), P("dp", None),
    )
    return jax.shard_map(
        on_device,
        mesh=mesh,
        in_specs=placed,
        out_specs=(
            P("dp", None), P("dp", None), P(None, None, "tensor"), P(None, "tensor"), P("tensor", None),
            P(), P(), P(), P(None, "tensor"), P("tensor"), P("tensor", None), P(), P(), P(),
        ),
        check_vma=False,
    )
```

time: 934 us -> 661 us (0.71)
  waiting for transfers between devices: 561 us -> 257 us
  Pallas kernels: 0 us -> 200 us
  matrix products: 109 us -> 3.41 us
  starting transfers between devices: 10.8 us -> 82 us
  local copies, waits for them, and re-layouts: 90.2 us -> 32.1 us
  blocking collectives: 86.4 us -> 52.1 us
  other arithmetic: 47.6 us -> 18.7 us
    pallas_call x0 -> x9, Pallas kernels: none -> 200 us  [the longest x1 40.4 us: attn_bwd(): pl.pallas_call(functools.partial(attn_bwd_kernel, lens.shape[0], 256, 256...]
    reduce_scatter x4 -> x6, waiting for transfers between devices: 268 us -> 70.2 us  [the longest x3 51.8 us: reduce_weight(): lax.psum_scatter(split, 'dp', scatter_dimension=0, axis_index_groups=octs...]
    dot_general x32 -> x1, matrix products: 107 us -> 3.41 us  [on_device(): jnp.einsum('td,cte->cde', xg, g3, preferred_element_type=F32).astype(BF)]
    psum x1, waiting for transfers between devices: 92.3 us -> 8.59 us  [on_device(): grad_w_qkv = lax.psum(dqkv, 'dp').astype(F32)]
    ppermute x0 -> x24, starting transfers between devices: none -> 81.3 us  [the longest x4 49.9 us: send_back(): got.append(lax.ppermute(pick, 'dp', perm))]
    ppermute x0 -> x24, waiting for transfers between devices: none -> 55.3 us  [the longest x12 27.6 us: on_device(): dpp = lambda x, k: lax.ppermute(x, 'dp', [(i, i ^ k) for i in range(G)])]
    all_gather x5 -> x4, waiting for transfers between devices: 173 us -> 122 us  [the longest x2 82.5 us: send_back(): return lax.all_gather(mine, 'tensor', axis=0, tiled=True)]
    all_to_all x2 -> x0, blocking collectives: 28.8 us -> none  [the longest x1 14.8 us: on_device(): lax.all_to_all(result.astype(jnp.bfloat16), 'dp', split_axis=0, concat_ax...]
  transfers between devices with their start and end apart: 12 -> 35, of which waited for: 10 -> 18; matrix products, arithmetic and copies ran while one was open for 5% -> 6% of each run, Pallas kernels for 0% -> 21%
where the time goes in v1:
time: 661 us; the launch traced here: 660 us
  waiting for transfers between devices  257 us (39%)
  Pallas kernels  200 us (30%)
  starting transfers between devices  82 us (12%)
  blocking collectives  52.1 us (8%)
  local copies, waits for them, and re-layouts  32.1 us (5%)
  other arithmetic  18.7 us (3%)
  between operations  14.4 us (2%)
    all_gather x2, waiting for transfers between devices, send_back(): return lax.all_gather(mine, 'tensor', axis=0, tiled=True)  82.5 us
    reduce_scatter x3, waiting for transfers between devices, reduce_weight(): lax.psum_scatter(split, 'dp', scatter_dimension=0, axis_index_groups=octs...  51.8 us
    ppermute x4, starting transfers between devices, send_back(): got.append(lax.ppermute(pick, 'dp', perm))  49.9 us
    psum x1, blocking collectives, on_device(): small = lax.psum(small, ('dp', 'tensor'))  42.5 us
    pallas_call x1, Pallas kernels, attn_bwd(): pl.pallas_call(functools.partial(attn_bwd_kernel, lens.shape[0], 256, 256...  40.4 us
    pallas_call x1, Pallas kernels, deal(): pl.pallas_call(functools.partial(deal_kernel, G), in_specs=[ANY] * 5, out...  40.1 us
    all_gather x2, waiting for transfers between devices, reduce_weight(): lax.all_gather(mine[0], 'dp', axis=0, axis_index_groups=octs, tiled=True)  39.4 us
    pallas_call x1, Pallas kernels, attn_fwd(): pl.pallas_call(functools.partial(attn_fwd_kernel, lens.shape[0], 256, 256...  33.6 us
  transfers between devices with their start and end apart: 35, of which 18 were waited for; matrix products, arithmetic and copies ran while one was open for 6% of the time, Pallas kernels for 21%

profile of v1, /device:TPU:0, one launch (start us, length us, event | category | flops | bytes accessed | tf_op | source)
XLA Modules:
  0.0 659.5 jit_solution(10769445818720702620)
XLA Ops:
  32.1 10.6 %collective-permute-done.1 = bf16[160,768]{1,0:T(8,128)(2,1)S(1)} collective-permute-done((bf16[160,768]{1,0:T(8,128)(2,1)S(1)}, bf16[160,768]{1,0:T(8,128)(2,1)S(1)}, u32[]{:S(2)}, u32[]{:S(2)}) %collective-permute-start.1) | collective-permute-done | bytes 245792 | tf_op jit(solution)/shard_map/ppermute | solution.py:727
  69.7 5.5 pick.1
  75.8 40.1 %deal.1 = (bf16[4,2,192,768]{3,2,1,0:T(8,128)(2,1)}, bf16[2,192,768]{2,1,0:T(8,128)(2,1)}, s32[8,128]{1,0:T(8,128)}, bf16[3,8,96,192]{3,2,1,0:T(8,128)(2,1)}, f32[8,192]{1,0:T(8,128)}) custom-call(bf16[2,192,768]{2,1,0:T(8,128)(2,1)} %bitcast.79, bf16[2,192,768]{2,1,0:T(8,128)(2,1)} %bitcast.80, s32[8,128]{1,0:T(8,128)} %scatter.12.len_ref, ...), custom_call_target="tpu_custom_call" | custom-call | tf_op jit(solution)/shard_map/deal/pallas_call | solution.py:239
  117.0 33.6 %attn_fwd.1 = (bf16[384,192]{1,0:T(8,128)(2,1)}, bf16[384,192]{1,0:T(8,128)(2,1)}, bf16[384,192]{1,0:T(8,128)(2,1)}, bf16[384,192]{1,0:T(8,128)(2,1)}, f32[1536,...) custom-call(s32[3]{0:T(128)} %slice_bitcast_fusion.sc_ref, ...), custom_call_target="tpu_custom_call" | custom-call | tf_op jit(solution)/shard_map/attn_fwd/pallas_call | solution.py:367
  150.6 25.0 %quad.1 = (bf16[384,192]{1,0:T(8,128)(2,1)}, bf16[384,192]{1,0:T(8,128)(2,1)}, bf16[384,192]{1,0:T(8,128)(2,1)}, bf16[3,160,768]{2,1,0:T(8,128)(2,1)}, bf16[3,16...) custom-call(bf16[384,192]{1,0:T(8,128)(2,1)} %get-tuple-element.94.r, ...), custom_call_target="tpu_custom_call" | custom-call | tf_op jit(solution)/shard_map/quad/pallas_call | solution.py:521
  175.6 25.4 %ffn.1 = (bf16[384,768]{1,0:T(8,128)(2,1)}, f32[384,768]{1,0:T(8,128)}, bf16[384,192]{1,0:T(8,128)(2,1)}, bf16[384,192]{1,0:T(8,128)(2,1)}, bf16[384,192]{1,0:T(...) custom-call(bf16[384,192]{1,0:T(8,128)(2,1)} %get-tuple-element.93.a, ...), custom_call_target="tpu_custom_call" | custom-call | tf_op jit(solution)/shard_map/ffn/pallas_call | solution.py:660
  201.0 13.3 %wgrad.1 = (bf16[4,768,768]{2,1,0:T(8,128)(2,1)}, bf16[4,768,768]{2,1,0:T(8,128)(2,1)}, bf16[4,192,768]{2,1,0:T(8,128)(2,1)}) custom-call(bf16[384,192]{1,0:T(8,128)(2,1)} %get-tuple-element.93.a0.o0, bf16[384,192]{1,0:T(8,128)(2,1)} %get-tuple-element.97.a1, bf16[384,192]{1,0:T(8,128)(2,1)} %get-tuple-element.98.a2, bf16[384,192]{1,0:T(8,128)(2,1)} %get-tuple-element.99.a3, ...), custom_call_target="tpu_custom_call" | custom-call | tf_op jit(solution)/shard_map/wgrad/pallas_call | solution.py:699
  226.7 46.6 %reduce-scatter.15.cloned.1.call-done = bf16[1,4,96,768]{3,2,1,0:T(8,128)(2,1)} async-done(((bf16[8,4,96,768]{3,2,1,0:T(8,128)(2,1)}), bf16[1,4,96,768]{3,2,1,0:T(8,128)(2,1)}) %reduce-scatter.15.cloned.1.call-update) | async-done | bytes 589840 | tf_op jit(solution)/shard_map/reduce_scatter | solution.py:795
  275.5 5.9 collective-permute-done.15.d2
  285.4 40.4 %attn_bwd.1 = (bf16[1536,192]{1,0:T(8,128)(2,1)}, bf16[1536,192]{1,0:T(8,128)(2,1)}, bf16[1536,192]{1,0:T(8,128)(2,1)}, bf16[384,768]{1,0:T(8,128)(2,1)}, bf16[3...) custom-call(s32[3]{0:T(128)} %slice_bitcast_fusion.sc_ref, ...), custom_call_target="tpu_custom_call" | custom-call | tf_op jit(solution)/shard_map/attn_bwd/pallas_call | solution.py:479
  337.1 45.3 %collective-permute-start.13 = (bf16[192,768]{1,0:T(8,128)(2,1)S(1)}, bf16[192,768]{1,0:T(8,128)(2,1)S(1)}, u32[]{:S(2)}, u32[]{:S(2)}) collective-permute-start(bf16[192,768]{1,0:T(8,128)(2,1)S(1)} %get-tuple-element.139), channel_id=1, source_target_pairs={{0,4},{4,12},{8,20},{12,28},{16,0},{20,8},{24,16},{28,24},{1,5},{5... | collective-permute-start | bytes 884744 | tf_op jit(solution)/shard_map/ppermute | solution.py:772
  384.5 5.6 collective-permute-start.18
  394.7 13.8 %collective-permute-done.19 = bf16[384,768]{1,0:T(8,128)(2,1)S(1)} collective-permute-done((bf16[384,768]{1,0:T(8,128)(2,1)S(1)}, bf16[384,768]{1,0:T(8,128)(2,1)S(1)}, u32[]{:S(2)}, u32[]{:S(2)}) %collective-permute-start.19) | collective-permute-done | bytes 589856 | tf_op jit(solution)/shard_map/ppermute | solution.py:726
  412.9 7.5 %collective-permute-done.21 = bf16[192,768]{1,0:T(8,128)(2,1)S(1)} collective-permute-done((bf16[192,768]{1,0:T(8,128)(2,1)S(1)}, bf16[192,768]{1,0:T(8,128)(2,1)S(1)}, u32[]{:S(2)}, u32[]{:S(2)}) %collective-permute-start.21) | collective-permute-done | bytes 294944 | tf_op jit(solution)/shard_map/ppermute | solution.py:772
  424.9 42.5 %psum.15 = f32[9216]{0:T(1024)S(1)} all-reduce(f32[9216]{0:T(1024)S(1)} %pad_maximum_fusion.5), channel_id=1, replica_groups=mesh['dp'=8,'tensor'=4] {'dp','tensor'}, use_global_device_ids=true, to_apply=%region_3.4 | all-reduce | flops 9216 | bytes 73728 | tf_op jit(solution)/shard_map/psum | solution.py:815
  468.9 8.6 %all-reduce.4.cloned.1.call-done = bf16[3,768,192]{1,2,0:T(8,128)(2,1)} async-done(((bf16[3,768,192]{1,2,0:T(8,128)(2,1)}), bf16[3,768,192]{1,2,0:T(8,128)(2,1)}) %all-reduce.4.cloned.1.call-update) | async-done | bytes 884752 | tf_op jit(solution)/shard_map/psum | solution.py:809
  480.0 18.3 %reduce-scatter.9.cloned.1.call-done = bf16[1,24,768]{2,1,0:T(8,128)(2,1)} async-done(((bf16[4,24,768]{2,1,0:T(8,128)(2,1)}), bf16[1,24,768]{2,1,0:T(8,128)(2,1)}) %reduce-scatter.9.cloned.1.call-update) | async-done | bytes 36880 | tf_op jit(solution)/shard_map/reduce_scatter | solution.py:798
  498.3 9.6 %all-gather = bf16[1,192,768]{2,1,0:T(8,128)(2,1)S(1)} all-gather(bf16[1,24,768]{2,1,0:T(8,128)(2,1)} %reduce-scatter.9.cloned.1.call-done), channel_id=2, replica_groups={{0,4,8,12,16,20,24,28},{1,5,9,13,17,21,25,29},{2,6,10,14,18,22,26,30},{..., dimensions={1}, use_global_device_ids=true | all-gather | bytes 331776 | tf_op jit(solution)/shard_map/all_gather | solution.py:799
  508.8 39.8 %all-gather.8.cloned.1.call-done.rows_ref = bf16[1536,768]{1,0:T(8,128)(2,1)} async-done(((bf16[384,768]{1,0:T(8,128)(2,1)}), bf16[1536,768]{1,0:T(8,128)(2,1)}) %all-gather.8.cloned.1.call-update) | async-done | bytes 2359312 | tf_op jit(solution)/shard_map/all_gather | solution.py:774
  548.6 8.2 %place.2 = bf16[1536,768]{1,0:T(8,128)(2,1)} custom-call(s32[1536,1]{1,0:T(8,128)} %reshape.192.row_ref, bf16[1536,768]{1,0:T(8,128)(2,1)} %all-gather.8.cloned.1.call-done.rows_ref), custom_call_target="tpu_custom_call" | custom-call | tf_op jit(solution)/shard_map/place/pallas_call | solution.py:82
  556.8 42.7 %all-gather.10.cloned.1.call-done.rows_ref = bf16[1536,768]{1,0:T(8,128)(2,1)} async-done(((bf16[384,768]{1,0:T(8,128)(2,1)}), bf16[1536,768]{1,0:T(8,128)(2,1)}) %all-gather.10.cloned.1.call-update) | async-done | bytes 2359312 | tf_op jit(solution)/shard_map/all_gather | solution.py:774
  599.5 8.2 %place.3 = bf16[1536,768]{1,0:T(8,128)(2,1)} custom-call(s32[1536,1]{1,0:T(8,128)} %reshape.192.row_ref, bf16[1536,768]{1,0:T(8,128)(2,1)} %all-gather.10.cloned.1.call-done.rows_ref), custom_call_target="tpu_custom_call" | custom-call | tf_op jit(solution)/shard_map/place/pallas_call | solution.py:82
  607.7 16.4 %all-gather.14.cloned.1.call-done = bf16[1,768,768]{2,1,0:T(8,128)(2,1)} async-done(((bf16[1,96,768]{2,1,0:T(8,128)(2,1)}), bf16[1,768,768]{2,1,0:T(8,128)(2,1)}) %all-gather.14.cloned.1.call-update) | async-done | bytes 1179664 | tf_op jit(solution)/shard_map/all_gather | solution.py:799
  627.1 23.0 %all-gather.12.cloned.1.call-done = bf16[1,768,768]{2,1,0:T(8,128)(2,1)} async-done(((bf16[1,96,768]{2,1,0:T(8,128)(2,1)}), bf16[1,768,768]{2,1,0:T(8,128)(2,1)}) %all-gather.12.cloned.1.call-update) | async-done | bytes 1179664 | tf_op jit(solution)/shard_map/all_gather | solution.py:799
  (171 shorter events, 109.3 us)
Async XLA Ops:
  7.2 266.0 %reduce-scatter.15.cloned.1.call-start = ((), (), s32[]{:S(2)}) async-start(), calls=%async_computation.13 | async-start | bytes 5308416 | tf_op jit(solution)/shard_map/reduce_scatter | solution.py:795
  8.4 12.8 %collective-permute-start.8 = (bf16[96,768]{1,0:T(8,128)(2,1)S(1)}, bf16[96,768]{1,0:T(8,128)(2,1)S(1)}, u32[]{:S(2)}, u32[]{:S(2)}) collective-permute-start(bf16[96,768]{1,0:T(8,128)(2,1)S(1)} %dynamic-slice_convert_fusion), channel_id=1, source_target_pairs={{0,3},{1,2},{2,1},{3,0},{4,7},{5,6},{6,5},{7,4},{8,11},{9,10},{10,... | collective-permute-start | bytes 442376 | tf_op jit(solution)/shard_map/ppermute | solution.py:727
  13.5 13.5 %collective-permute-start.7 = (bf16[96,768]{1,0:T(8,128)(2,1)S(1)}, bf16[96,768]{1,0:T(8,128)(2,1)S(1)}, u32[]{:S(2)}, u32[]{:S(2)}) collective-permute-start(bf16[96,768]{1,0:T(8,128)(2,1)S(1)} %dynamic-slice_convert_fusion), channel_id=1, source_target_pairs={{0,2},{1,3},{2,0},{3,1},{4,6},{5,7},{6,4},{7,5},{8,10},{9,11},{10,... | collective-permute-start | bytes 442376 | tf_op jit(solution)/shard_map/ppermute | solution.py:727
  16.8 15.3 %collective-permute-start = (bf16[160,768]{1,0:T(8,128)(2,1)S(1)}, bf16[160,768]{1,0:T(8,128)(2,1)S(1)}, u32[]{:S(2)}, u32[]{:S(2)}) collective-permute-start(bf16[160,768]{1,0:T(8,128)(2,1)S(1)} %pad_maximum_fusion.4), channel_id=1, source_target_pairs={{0,1},{1,0},{2,3},{3,2},{4,5},{5,4},{6,7},{7,6},{8,9},{9,8},{10,11... | collective-permute-start | bytes 737288 | tf_op jit(solution)/shard_map/ppermute | solution.py:727
  18.2 24.5 %collective-permute-start.1 = (bf16[160,768]{1,0:T(8,128)(2,1)S(1)}, bf16[160,768]{1,0:T(8,128)(2,1)S(1)}, u32[]{:S(2)}, u32[]{:S(2)}) collective-permute-start(bf16[160,768]{1,0:T(8,128)(2,1)S(1)} %pad_maximum_fusion.4), channel_id=1, source_target_pairs={{0,2},{1,3},{2,0},{3,1},{4,6},{5,7},{6,4},{7,5},{8,10},{9,11},{10,... | collective-permute-start | bytes 737288 | tf_op jit(solution)/shard_map/ppermute | solution.py:727
  21.2 21.6 %collective-permute-start.2 = (bf16[160,768]{1,0:T(8,128)(2,1)S(1)}, bf16[160,768]{1,0:T(8,128)(2,1)S(1)}, u32[]{:S(2)}, u32[]{:S(2)}) collective-permute-start(bf16[160,768]{1,0:T(8,128)(2,1)S(1)} %pad_maximum_fusion.4), channel_id=1, source_target_pairs={{0,3},{1,2},{2,1},{3,0},{4,7},{5,6},{6,5},{7,4},{8,11},{9,10},{10,... | collective-permute-start | bytes 737288 | tf_op jit(solution)/shard_map/ppermute | solution.py:727
  27.1 25.2 %collective-permute-start.9 = (bf16[3,96,768]{2,1,0:T(8,128)(2,1)S(1)}, bf16[3,96,768]{2,1,0:T(8,128)(2,1)S(1)}, u32[]{:S(2)}, u32[]{:S(2)}) collective-permute-start(bf16[3,96,768]{2,1,0:T(8,128)(2,1)S(1)} %pad_maximum_fusion.3.refs_7_.z2), channel_id=1, source_target_pairs={{0,8},{4,12},{8,0},{12,4},{16,24},{20,28},{24,16},{28,20},{1,9},{5... | collective-permute-start | bytes 1327112 | tf_op jit(solution)/shard_map/ppermute | solution.py:726
  45.3 105.3 %collective-permute-start.3 = (bf16[3,160,768]{2,1,0:T(8,128)(2,1)S(1)}, bf16[3,160,768]{2,1,0:T(8,128)(2,1)}, u32[]{:S(2)}, u32[]{:S(2)}) collective-permute-start(bf16[3,160,768]{2,1,0:T(8,128)(2,1)S(1)} %pad_maximum_fusion.refs_3_.z1), channel_id=1, source_target_pairs={{0,8},{4,12},{8,0},{12,4},{16,24},{20,28},{24,16},{28,20},{1,9},{5... | collective-permute-start | bytes 2211848 | tf_op jit(solution)/shard_map/ppermute | solution.py:726
  51.7 98.9 %collective-permute-start.10 = (bf16[3,96,768]{2,1,0:T(8,128)(2,1)S(1)}, bf16[3,96,768]{2,1,0:T(8,128)(2,1)}, u32[]{:S(2)}, u32[]{:S(2)}) collective-permute-start(bf16[3,96,768]{2,1,0:T(8,128)(2,1)S(1)} %pad_maximum_fusion.3.refs_7_.z2), channel_id=1, source_target_pairs={{0,16},{4,20},{8,24},{12,28},{16,0},{20,4},{24,8},{28,12},{1,17},{... | collective-permute-start | bytes 1327112 | tf_op jit(solution)/shard_map/ppermute | solution.py:726
  52.2 98.4 %collective-permute-start.11 = (bf16[3,96,768]{2,1,0:T(8,128)(2,1)S(1)}, bf16[3,96,768]{2,1,0:T(8,128)(2,1)}, u32[]{:S(2)}, u32[]{:S(2)}) collective-permute-start(bf16[3,96,768]{2,1,0:T(8,128)(2,1)S(1)} %collective-permute-done.9.refs_8_.c2), channel_id=1, source_target_pairs={{0,16},{4,20},{8,24},{12,28},{16,0},{20,4},{24,8},{28,12},{1,17},{... | collective-permute-start | bytes 1327112 | tf_op jit(solution)/shard_map/ppermute | solution.py:726
  56.5 94.1 %collective-permute-start.5 = (bf16[3,96,768]{2,1,0:T(8,128)(2,1)}, bf16[3,96,768]{2,1,0:T(8,128)(2,1)}, u32[]{:S(2)}, u32[]{:S(2)}) collective-permute-start(bf16[3,96,768]{2,1,0:T(8,128)(2,1)} %collective-permute-done.4.refs_5_.y1), channel_id=1, source_target_pairs={{0,8},{4,12},{8,0},{12,4},{16,24},{20,28},{24,16},{28,20},{1,9},{5... | collective-permute-start | bytes 1327112 | tf_op jit(solution)/shard_map/ppermute | solution.py:726
  219.2 111.8 %reduce-scatter.11.cloned.1.call-start = ((), (), s32[]{:S(2)}) async-start(), calls=%async_computation.11 | async-start | bytes 5308416 | tf_op jit(solution)/shard_map/reduce_scatter | solution.py:795
  224.1 158.2 %reduce-scatter.7.cloned.1.call-start = ((), (), s32[]{:S(2)}) async-start(), calls=%async_computation.9 | async-start | bytes 1327104 | tf_op jit(solution)/shard_map/reduce_scatter | solution.py:795
  226.6 194.8 %reduce-scatter.17.cloned.1.call-start = ((), (), s32[]{:S(2)}) async-start(), calls=%async_computation.14 | async-start | bytes 737280 | tf_op jit(solution)/shard_map/reduce_scatter | solution.py:798
  273.2 148.7 %reduce-scatter.13.cloned.1.call-start = ((), (), s32[]{:S(2)}) async-start(), calls=%async_computation.12 | async-start | bytes 737280 | tf_op jit(solution)/shard_map/reduce_scatter | solution.py:798
  331.0 146.4 %all-reduce.4.cloned.1.call-start = ((), (), s32[]{:S(2)}) async-start(), calls=%async_computation.8 | async-start | bytes 1769472 | tf_op jit(solution)/shard_map/psum | solution.py:809
  336.2 162.1 %reduce-scatter.9.cloned.1.call-start = ((), (), s32[]{:S(2)}) async-start(), calls=%async_computation.10 | async-start | bytes 184320 | tf_op jit(solution)/shard_map/reduce_scatter | solution.py:798
  336.4 46.0 %collective-permute-start.12 = (bf16[192,768]{1,0:T(8,128)(2,1)S(1)}, bf16[192,768]{1,0:T(8,128)(2,1)S(1)}, u32[]{:S(2)}, u32[]{:S(2)}) collective-permute-start(bf16[192,768]{1,0:T(8,128)(2,1)S(1)} %get-tuple-element.138), channel_id=1, source_target_pairs={{0,0},{4,8},{8,16},{12,24},{16,4},{20,12},{24,20},{28,28},{1,1},{5... | collective-permute-start | bytes 884744 | tf_op jit(solution)/shard_map/ppermute | solution.py:772
  337.1 46.5 %collective-permute-start.13 = (bf16[192,768]{1,0:T(8,128)(2,1)S(1)}, bf16[192,768]{1,0:T(8,128)(2,1)S(1)}, u32[]{:S(2)}, u32[]{:S(2)}) collective-permute-start(bf16[192,768]{1,0:T(8,128)(2,1)S(1)} %get-tuple-element.139), channel_id=1, source_target_pairs={{0,4},{4,12},{8,20},{12,28},{16,0},{20,8},{24,16},{28,24},{1,5},{5... | collective-permute-start | bytes 884744 | tf_op jit(solution)/shard_map/ppermute | solution.py:772
  382.4 166.2 %all-gather.8.cloned.1.call-start = ((), (), s32[]{:S(2)}) async-start(), calls=%async_computation.6 | async-start | bytes 2949120 | tf_op jit(solution)/shard_map/all_gather | solution.py:774
  384.4 215.1 %all-gather.10.cloned.1.call-start = ((), (), s32[]{:S(2)}) async-start(), calls=%async_computation.7 | async-start | bytes 2949120 | tf_op jit(solution)/shard_map/all_gather | solution.py:774
  392.1 16.5 %collective-permute-start.19 = (bf16[384,768]{1,0:T(8,128)(2,1)S(1)}, bf16[384,768]{1,0:T(8,128)(2,1)S(1)}, u32[]{:S(2)}, u32[]{:S(2)}) collective-permute-start(bf16[384,768]{1,0:T(8,128)(2,1)S(1)} %add_convert_fusion.1), channel_id=1, source_target_pairs={{0,8},{4,12},{8,0},{12,4},{16,24},{20,28},{24,16},{28,20},{1,9},{5... | collective-permute-start | bytes 1769480 | tf_op jit(solution)/shard_map/ppermute | solution.py:726
  421.3 202.8 %all-gather.14.cloned.1.call-start = ((), (), s32[]{:S(2)}) async-start(), calls=%async_computation.16 | async-start | bytes 1327104 | tf_op jit(solution)/shard_map/all_gather | solution.py:799
  421.9 228.2 %all-gather.12.cloned.1.call-start = ((), (), s32[]{:S(2)}) async-start(), calls=%async_computation.15 | async-start | bytes 1327104 | tf_op jit(solution)/shard_map/all_gather | solution.py:799
  (37 other events, 591.6 us)
Sparse Core Ops, SparseCore 0:
  219.3 53.8 reduce-scatter.14
  277.1 53.9 reduce-scatter.10
  334.8 37.4 reduce-scatter.6
  374.5 22.0 reduce-scatter.16
  398.8 20.2 reduce-scatter.12
  423.1 54.3 all-reduce.3
  479.8 18.4 reduce-scatter.8
  499.9 48.6 all-gather.7
  550.2 49.2 all-gather.9
  601.2 22.8 all-gather.13
  626.0 24.0 all-gather.11
